TPU v7x, 32 devices: a whole 2x2x4 slice. The times are simulated.
32 devices in a mesh: groups: 2 (over y), ctx: 4 (over z), tensor: 2 (over x), dp: 2 (over core).
Axes of the slice: x: 2, y: 2, z: 4, core: 2. Of those that a mesh axis runs over, the one named last changes fastest.
Arguments:
- tokens: bfloat16 [4, 1024, 1024], P(('groups', 'dp'), 'ctx', 'tensor'), parts along dimension 0
- w_qkv: bfloat16 [1024, 3, 1024], P(None, None, 'tensor')
- w_out: bfloat16 [1024, 1024], P('tensor'), may hold values from -0.1875 to 0.1875
- labels: int32 [4, 8, 1024], P(('groups', 'dp'), 'tensor', 'ctx'), parts along dimension 0, may hold values from 0 to 255, as said below
- grad_out: bfloat16 [4, 1024, 1024], P(('groups', 'dp'), 'ctx', 'tensor'), parts along dimension 0, may hold values from -6 to 6
Outputs:
- attended: bfloat16 [4, 1024, 1024], P(('groups', 'dp'), 'ctx', 'tensor'), parts along dimension 0
- grad_tokens: bfloat16 [4, 1024, 1024], P(('groups', 'dp'), 'ctx', 'tensor'), parts along dimension 0
- grad_w_qkv: float32 [2048, 3, 1024], P('groups', None, 'tensor'), parts along dimension 0
- grad_w_out: float32 [2048, 1024], P(('groups', 'tensor')), parts along dimension 0
There are 2 independent parts, one for each index of `groups`. A program takes and returns all parts, laid end to end along the dimension named above; an argument that names none is the same for every part. Nothing has to cross between parts.
Inputs may be any that keep to these rules, and one draw needn't show every extreme that they name: `labels`: cluster c of any head belongs to owner c % 4. Among the 256 tokens of one document on one index of ctx, at most 192 have, for one head, clusters of one owner; for each head one owner has exactly 192 from every such block, and the other owners share the rest of a block evenly (counts differ by at most one).
All inputs are finite; a program needn't handle non-finite values.
Results may differ from a plain program's by a relative error of at most 0.035.
The roundings to bfloat16 on the way count: a program that leaves them out, or rounds other values in their place, can miss the bound.
Values may be sent and summed in bfloat16 or wider, within the bound.
A program may use at most 64 MiB of HBM per device.

v0:
```python
import math

import jax
import jax.numpy as jnp
from jax import lax
from jax.sharding import PartitionSpec as P

HD = 128


def contract_last(left, right):
    return lax.dot_general(
        left, right, (((1,), (1,)), ((), ())), preferred_element_type=jnp.float32
    )


def contract_first(left, right):
    return lax.dot_general(
        left, right, (((0,), (0,)), ((), ())), preferred_element_type=jnp.float32
    )


def masked_probs(query_block, label_block, keys_in, marks):
    scores = contract_last(query_block, keys_in) * HD ** (-0.5)
    same = label_block[:, None] == marks[None, :]
    scores = jnp.where(same, scores, jnp.float32(-1e30))
    top_value = jnp.max(scores, axis=1, keepdims=True)
    expo = jnp.exp(scores - top_value)
    return expo / jnp.sum(expo, axis=1, keepdims=True)


def owner_forward(queries, keys_in, values_in, marks):
    total = queries.shape[0]
    block_rows = math.gcd(total, 512)
    block_count = total // block_rows

    def forward_block(index):
        start = index * block_rows
        query_block = lax.dynamic_slice_in_dim(queries, start, block_rows, 0)
        label_block = lax.dynamic_slice_in_dim(marks, start, block_rows, 0)
        probs = masked_probs(query_block, label_block, keys_in, marks).astype(jnp.bfloat16)
        return jnp.dot(probs, values_in, preferred_element_type=jnp.float32).astype(jnp.bfloat16)

    return lax.map(forward_block, jnp.arange(block_count, dtype=jnp.int32)).reshape(
        total, queries.shape[1]
    )


def owner_backward(queries, keys_in, values_in, marks, attention, cotangent):
    total, size = queries.shape
    block_rows = math.gcd(total, 512)
    block_count = total // block_rows

    def backward_block(carry, index):
        grad_keys, grad_values = carry
        start = index * block_rows
        query_block = lax.dynamic_slice_in_dim(queries, start, block_rows, 0)
        label_block = lax.dynamic_slice_in_dim(marks, start, block_rows, 0)
        attn_block = lax.dynamic_slice_in_dim(attention, start, block_rows, 0)
        cot_block = lax.dynamic_slice_in_dim(cotangent, start, block_rows, 0)
        probs_full = masked_probs(query_block, label_block, keys_in, marks)
        probs = probs_full.astype(jnp.bfloat16)
        dprob = contract_last(cot_block, values_in)
        delta = jnp.sum(
            cot_block.astype(jnp.float32) * attn_block.astype(jnp.float32), axis=1, keepdims=True
        )
        dscore = (probs_full * (dprob - delta) * HD ** (-0.5)).astype(jnp.bfloat16)
        grad_query = jnp.dot(dscore, keys_in, preferred_element_type=jnp.float32).astype(
            jnp.bfloat16
        )
        grad_keys = grad_keys + contract_first(dscore, query_block)
        grad_values = grad_values + contract_first(probs, cot_block)
        return ((grad_keys, grad_values), grad_query)

    empty = jnp.zeros((total, size), jnp.float32)
    (grad_keys, grad_values), grad_queries = lax.scan(
        backward_block, (empty, empty), jnp.arange(block_count, dtype=jnp.int32)
    )
    return (
        grad_queries.reshape(total, size),
        grad_keys.astype(jnp.bfloat16),
        grad_values.astype(jnp.bfloat16),
    )


def shards(tokens, w_qkv, w_out, labels, grad_out):
    rows_all, grads_all = (
        lax.all_gather(tokens, "tensor", axis=2, tiled=True),
        lax.all_gather(grad_out, "tensor", axis=2, tiled=True),
    )
    tok_rows = rows_all[0]
    tok_grads = grads_all[0]
    tok_count, width = tok_rows.shape
    heads_local = w_out.shape[0] // HD
    ctx_count = lax.axis_size("ctx")
    capacity = 3 * tok_count // ctx_count
    slot_total = ctx_count * capacity
    qkv = jnp.dot(
        tok_rows, w_qkv.reshape(width, 3 * heads_local * HD), preferred_element_type=jnp.float32
    )
    qkv = qkv.astype(jnp.bfloat16).reshape(tok_count, 3, heads_local, HD)
    qkv_heads = jnp.transpose(qkv, (2, 0, 1, 3)).reshape(heads_local, tok_count, 3 * HD)
    cotangent = contract_last(tok_grads, w_out).astype(jnp.bfloat16)
    cot_heads = jnp.transpose(cotangent.reshape(tok_count, heads_local, HD), (1, 0, 2))
    labels_local = labels[0]
    owner_of = labels_local % ctx_count
    owner_hits = (
        owner_of[:, :, None] == jnp.arange(ctx_count, dtype=jnp.int32)[None, None, :]
    ).astype(jnp.int32)
    earlier = jnp.cumsum(owner_hits, axis=1) - owner_hits
    slot_index = jnp.sum(earlier * owner_hits, axis=2)
    destination = owner_of * capacity + slot_index

    def pack(values):
        feature_count = values.shape[2]
        empty_buffer = jnp.zeros((heads_local, slot_total, feature_count), values.dtype)
        filled = jax.vmap(lambda buffer, where_to, rows_in: buffer.at[where_to].set(rows_in))(
            empty_buffer, destination, values
        )
        return filled.reshape(heads_local, ctx_count, capacity, feature_count)

    def unpack(received):
        flat = received.reshape(heads_local, slot_total, received.shape[3])
        return jax.vmap(lambda table, where_to: jnp.take(table, where_to, axis=0))(
            flat, destination
        )

    label_slots = jax.vmap(
        lambda where_to, marks: jnp.full((slot_total,), -1.0, jnp.bfloat16).at[where_to].set(marks)
    )(destination, labels_local.astype(jnp.bfloat16)).reshape(heads_local, ctx_count, capacity)
    arrived, arrived_marks = (
        lax.all_to_all(pack(qkv_heads), "ctx", split_axis=1, concat_axis=1, tiled=True),
        lax.all_to_all(label_slots, "ctx", split_axis=1, concat_axis=1, tiled=True),
    )
    arrived = arrived.reshape(heads_local, slot_total, 3 * HD)
    marks_own = arrived_marks.reshape(heads_local, slot_total)
    queries_own = arrived[:, :, :HD]
    keys_own = arrived[:, :, HD : 2 * HD]
    values_own = arrived[:, :, 2 * HD :]
    attention_own = jax.vmap(owner_forward)(queries_own, keys_own, values_own, marks_own)
    returned = lax.all_to_all(
        attention_own.reshape(heads_local, ctx_count, capacity, HD),
        "ctx",
        split_axis=1,
        concat_axis=1,
        tiled=True,
    )
    attention_tok = unpack(returned)
    cot_arrived = lax.all_to_all(pack(cot_heads), "ctx", split_axis=1, concat_axis=1, tiled=True)
    cot_own = cot_arrived.reshape(heads_local, slot_total, HD)
    grad_q, grad_k, grad_v = jax.vmap(owner_backward)(
        queries_own, keys_own, values_own, marks_own, attention_own, cot_own
    )
    grads_own = jnp.concatenate([grad_q, grad_k, grad_v], axis=2).reshape(
        heads_local, ctx_count, capacity, 3 * HD
    )
    grads_back = lax.all_to_all(grads_own, "ctx", split_axis=1, concat_axis=1, tiled=True)
    grad_heads = unpack(grads_back)
    attention_rows = jnp.transpose(attention_tok, (1, 0, 2)).reshape(tok_count, heads_local * HD)
    out_terms = jnp.dot(attention_rows, w_out, preferred_element_type=jnp.float32)
    attended = lax.psum_scatter(
        out_terms.astype(jnp.bfloat16), "tensor", scatter_dimension=1, tiled=True
    )
    grad_qkv = jnp.transpose(grad_heads.reshape(heads_local, tok_count, 3, HD), (1, 2, 0, 3))
    grad_qkv = grad_qkv.reshape(tok_count, 3 * heads_local * HD)
    grad_w_out_local = contract_first(attention_rows, tok_grads)
    grad_w_qkv_local = contract_first(tok_rows, grad_qkv).reshape(width, 3, heads_local * HD)
    summed_qkv, summed_out = (
        lax.psum(grad_w_qkv_local.astype(jnp.bfloat16), ("ctx", "dp")).astype(jnp.float32),
        lax.psum(grad_w_out_local.astype(jnp.bfloat16), ("ctx", "dp")).astype(jnp.float32),
    )
    in_terms = contract_last(grad_qkv, w_qkv.reshape(width, 3 * heads_local * HD))
    grad_tokens = lax.psum_scatter(
        in_terms.astype(jnp.bfloat16), "tensor", scatter_dimension=1, tiled=True
    )
    return (attended[None], grad_tokens[None], summed_qkv, summed_out)


def solution(mesh):
    placed = (
        P(("groups", "dp"), "ctx", "tensor"),
        P(None, None, "tensor"),
        P("tensor", None),
        P(("groups", "dp"), "tensor", "ctx"),
        P(("groups", "dp"), "ctx", "tensor"),
    )
    return jax.shard_map(
        shards,
        mesh=mesh,
        in_specs=placed,
        out_specs=(
            P(("groups", "dp"), "ctx", "tensor"),
            P(("groups", "dp"), "ctx", "tensor"),
            P("groups", None, "tensor"),
            P(("groups", "tensor"), None),
        ),
        check_vma=False,
    )
```

profile of v0, /device:TPU:0, one launch (start us, length us, event | category | flops | bytes accessed | tf_op | source)
XLA Modules:
  0.0 419.2 jit_solution(18375576288930993019)
XLA Ops:
  10.2 4.8 %reduce-window.6 = s32[4,4,2,128]{3,2,1,0:T(2,128)S(1)} reduce-window(s32[4,4,2,128]{3,2,1,0:T(2,128)S(1)} %compare_convert_fusion, s32[]{:T(128)} %constant.96.clone.1), window={size=1x1x1x128 pad=0_0x0_0x0_0x127_0}, to_apply=%region_0.1 | reduce-window | flops 520192 | bytes 32772 | tf_op jit(solution)/shard_map/reduce-window
  17.8 7.6 %scatter_custom_fusion = bf16[3072]{0:T(1024)(128)(2,1)S(1)} fusion(s32[1024]{0:T(1024)S(1)} %bitcast.228, bf16[1024]{0:T(1024)(128)(2,1)S(1)} %bitcast.231, bf16[]{:T(256)} %constant.103.clone.1), kind=kCustom, calls=%fused_computation.120 | custom fusion | bytes 6146
  26.1 6.3 %all-to-all-start = ((bf16[4,4,192]{2,0,1:T(4,128)(2,1)}), bf16[4,4,192]{2,0,1:T(4,128)(2,1)S(1)}, u32[]{:S(2)}, u32[]{:S(2)}) async-start(bf16[4,4,192]{2,0,1:T(4,128)(2,1)} %copy.67), calls=%async_computation | async-start | bytes 16384 | tf_op jit(solution)/shard_map/all_to_all | solution.py:133
  32.4 8.6 %all_gather.7 = bf16[1,256,1024]{2,1,0:T(8,128)(2,1)S(1)} all-gather(bf16[1,256,512]{2,1,0:T(8,128)(2,1)} %param.13), channel_id=1, replica_groups=mesh['groups'=2,'ctx'=4,'tensor'=2,'dp'=2] {'tensor'}, dimensions={2}, use_global_device_ids=true | all-gather | bytes 786432 | tf_op jit(solution)/shard_map/all_gather | solution.py:89
  46.8 4.8 %all-to-all-start.3 = ((bf16[4,4,192,128]{3,2,0,1:T(8,128)(2,1)}), bf16[4,4,192,128]{3,2,0,1:T(8,128)(2,1)}, u32[]{:S(2)}, u32[]{:S(2)}) async-start(bf16[4,4,192,128]{3,2,0,1:T(8,128)(2,1)} %copy.80), calls=%async_computation.4 | async-start | bytes 1572864 | tf_op jit(solution)/shard_map/all_to_all | solution.py:149
  51.6 4.7 %copy.69 = bf16[1024,3,512]{0,2,1:T(8,128)(2,1)} copy(bf16[1024,3,512]{2,0,1:T(8,128)(2,1)} %param.10) | data formatting | bytes 6291456 | tf_op args[1]
  56.3 7.0 %all_gather.6 = bf16[1,256,1024]{2,1,0:T(8,128)(2,1)S(1)} all-gather(bf16[1,256,512]{2,1,0:T(8,128)(2,1)S(1)} %copy-done.10), channel_id=1, replica_groups=mesh['groups'=2,'ctx'=4,'tensor'=2,'dp'=2] {'tensor'}, dimensions={2}, use_global_device_ids=true | all-gather | bytes 786432 | tf_op jit(solution)/shard_map/all_gather | solution.py:88
  69.3 6.5 %scatter_custom_fusion.1 = bf16[3072,384]{1,0:T(8,128)(2,1)S(1)} fusion(s32[1024]{0:T(1024)S(1)} %bitcast.230, bf16[1024,384]{1,0:T(8,128)(2,1)} %copy.71, bf16[]{:T(256)} %constant.102.clone.1), kind=kCustom, calls=%fused_computation.77 | custom fusion | bytes 2359808
  77.5 5.1 %all-to-all-start.1 = ((bf16[4,4,192,384]{3,2,0,1:T(8,128)(2,1)}), bf16[4,4,192,384]{3,2,0,1:T(8,128)(2,1)}, u32[]{:S(2)}, u32[]{:S(2)}) async-start(bf16[4,4,192,384]{3,2,0,1:T(8,128)(2,1)} %copy.72), calls=%async_computation.1 | async-start | bytes 4718592 | tf_op jit(solution)/shard_map/all_to_all | solution.py:132
  85.0 48.7 %all-to-all-done.1 = bf16[4,4,192,384]{3,2,0,1:T(8,128)(2,1)} async-done(((bf16[4,4,192,384]{3,2,0,1:T(8,128)(2,1)}), bf16[4,4,192,384]{3,2,0,1:T(8,128)(2,1)}, u32[]{:S(2)}, u32[]{:S(2)}) %all-to-all-start.1) | async-done | bytes 2359328 | tf_op jit(solution)/shard_map/all_to_all | solution.py:132
  137.4 23.0 %while.33 = (s32[]{:T(128)}, bf16[3,4,256,128]{3,2,0,1:T(8,128)(2,1)S(1)}, s32[3]{0:T(128)S(1)}, bf16[4,768]{1,0:T(4,128)(2,1)S(1)}, bf16[4,4,192]{2,1,0:T(4,128...) while((s32[]{:T(128)}, ...), condition=%wide.wide.region_8.9_spmd, body=%wide.wide.region_5.8_spmd.sunk | while | flops 612764160 | bytes 3175139 | solution.py:44
  161.4 4.2 all-to-all-start.2
  166.7 56.3 %while.34 = (s32[]{:T(128)}, f32[4,768,128]{2,1,0:T(8,128)S(1)}, f32[4,768,128]{2,1,0:T(8,128)}, bf16[3,4,256,128]{3,2,0,1:T(8,128)(2,1)}, s32[3]{0:T(128)S(1)},...) while((s32[]{:T(128)}, f32[4,768,128]{2,1,0:T(8,128)S(1)}, ...), condition=%wide.wide.region_15.16_spmd.clone, body=%wide.wide.region_11.15_spmd.clone.sunk | while | flops 1222772224 | bytes 25732404 | solution.py:76
  169.2 4.1 fusion.187
  179.9 5.2 %select_add_fusion.7 = f32[4,768,128]{2,1,0:T(8,128)} fusion(f32[4,768,128]{2,1,0:T(8,128)} %get-tuple-element.590, f32[4,256]{1,0:T(4,128)S(1)} %get-tuple-element.527, pred[]{:T(512)S(6)} %compare.29, bf16[4,768,128]{2,1,0:T(8,128)(2,1)} %get-tuple-element.615, s32[]{:T(128)S(1)} %bitcast.226, ...), kind=kOutput, calls=%fused_computation.37.clone.clone.1 | convolution fusion | flops 408160000 | bytes 4469761 | tf_op jit(solution)/shard_map/vmap()/while/body/eval_jaxpr/dot_general | solution.py:18
  187.6 4.1 fusion.187
  198.3 5.7 %select_add_fusion.7 = f32[4,768,128]{2,1,0:T(8,128)} fusion(f32[4,768,128]{2,1,0:T(8,128)} %get-tuple-element.590, f32[4,256]{1,0:T(4,128)S(1)} %get-tuple-element.527, pred[]{:T(512)S(6)} %compare.29, bf16[4,768,128]{2,1,0:T(8,128)(2,1)} %get-tuple-element.615, s32[]{:T(128)S(1)} %bitcast.226, ...), kind=kOutput, calls=%fused_computation.37.clone.clone.1 | convolution fusion | flops 408160000 | bytes 4469761 | tf_op jit(solution)/shard_map/vmap()/while/body/eval_jaxpr/dot_general | solution.py:18
  217.2 5.7 %select_add_fusion.7 = f32[4,768,128]{2,1,0:T(8,128)} fusion(f32[4,768,128]{2,1,0:T(8,128)} %get-tuple-element.590, f32[4,256]{1,0:T(4,128)S(1)} %get-tuple-element.527, pred[]{:T(512)S(6)} %compare.29, bf16[4,768,128]{2,1,0:T(8,128)(2,1)} %get-tuple-element.615, s32[]{:T(128)S(1)} %bitcast.226, ...), kind=kOutput, calls=%fused_computation.37.clone.clone.1 | convolution fusion | flops 408160000 | bytes 4469761 | tf_op jit(solution)/shard_map/vmap()/while/body/eval_jaxpr/dot_general | solution.py:18
  227.6 5.2 %all-to-all-start.4 = ((bf16[4,4,192,384]{3,2,0,1:T(8,128)(2,1)}), bf16[4,4,192,384]{3,2,0,1:T(8,128)(2,1)}, u32[]{:S(2)}, u32[]{:S(2)}) async-start(bf16[4,4,192,384]{3,2,0,1:T(8,128)(2,1)} %copy.84), calls=%async_computation.5 | async-start | bytes 4718592 | tf_op jit(solution)/shard_map/all_to_all | solution.py:157
  234.1 5.8 %gather_fusion = bf16[1024,128]{1,0:T(8,128)(2,1)S(1)} fusion(bf16[4,768,128]{2,1,0:T(8,128)(2,1)S(1)} %bitcast.205, s32[1024]{0:T(1024)S(1)} %bitcast.199), kind=kCustom, calls=%fused_computation | custom fusion | bytes 532480 | tf_op jit(solution)/shard_map/vmap(jit(_take))/gather | solution.py:124
  242.3 43.4 %all-to-all-done.4 = bf16[4,4,192,384]{3,2,0,1:T(8,128)(2,1)} async-done(((bf16[4,4,192,384]{3,2,0,1:T(8,128)(2,1)}), bf16[4,4,192,384]{3,2,0,1:T(8,128)(2,1)}, u32[]{:S(2)}, u32[]{:S(2)}) %all-to-all-start.4) | async-done | bytes 2359328 | tf_op jit(solution)/shard_map/all_to_all | solution.py:157
  287.6 11.6 %gather_fusion.1 = bf16[1024,384]{1,0:T(8,128)(2,1)} fusion(bf16[4,768,384]{2,1,0:T(8,128)(2,1)S(1)} %bitcast.201, s32[1024]{0:T(1024)S(1)} %bitcast.200), kind=kCustom, calls=%fused_computation.1 | custom fusion | bytes 1581056 | tf_op jit(solution)/shard_map/vmap(jit(_take))/gather | solution.py:124
  304.4 4.7 %copy.88 = bf16[1024,3,512]{2,0,1:T(8,128)(2,1)} copy(bf16[1024,3,512]{0,2,1:T(8,128)(2,1)} %bitcast.202) | data formatting | bytes 6291456 | tf_op jit(solution)/shard_map/convert_element_type | solution.py:169
  315.1 90.2 %all-reduce.3.cloned.1.call-done = (bf16[1024,3,512]{2,0,1:T(8,128)(2,1)}, bf16[512,1024]{1,0:T(8,128)(2,1)}) async-done(((bf16[1024,3,512]{2,0,1:T(8,128)(2,1)}, bf16[512,1024]{1,0:T(8,128)(2,1)}), (bf16[1024,3,512]{2,0,1:T(8,128)(2,1)}, bf16[512,1024]{1,0:T(8,128)(2,1)})) %all-reduce.3.cloned.1.call-update) | async-done | bytes 4194320 | tf_op jit(solution)/shard_map/psum | solution.py:169
  (144 shorter events, 105.3 us)
Async XLA Ops:
  8.0 33.8 %copy-start = (bf16[512,1024]{1,0:T(8,128)(2,1)S(1)}, bf16[512,1024]{1,0:T(8,128)(2,1)}, u32[]{:S(2)}) copy-start(bf16[512,1024]{1,0:T(8,128)(2,1)} %param.11) | copy-start | bytes 3145732
  26.1 20.7 %all-to-all-start = ((bf16[4,4,192]{2,0,1:T(4,128)(2,1)}), bf16[4,4,192]{2,0,1:T(4,128)(2,1)S(1)}, u32[]{:S(2)}, u32[]{:S(2)}) async-start(bf16[4,4,192]{2,0,1:T(4,128)(2,1)} %copy.67), calls=%async_computation | async-start | bytes 16384 | tf_op jit(solution)/shard_map/all_to_all | solution.py:133
  41.0 0.8 copy-start.1
  46.8 30.7 %all-to-all-start.3 = ((bf16[4,4,192,128]{3,2,0,1:T(8,128)(2,1)}), bf16[4,4,192,128]{3,2,0,1:T(8,128)(2,1)}, u32[]{:S(2)}, u32[]{:S(2)}) async-start(bf16[4,4,192,128]{3,2,0,1:T(8,128)(2,1)} %copy.80), calls=%async_computation.4 | async-start | bytes 1572864 | tf_op jit(solution)/shard_map/all_to_all | solution.py:149
  51.6 4.7 %copy-start.10 = (bf16[1,256,512]{2,1,0:T(8,128)(2,1)S(1)}, bf16[1,256,512]{2,1,0:T(8,128)(2,1)}, u32[]{:S(2)}) copy-start(bf16[1,256,512]{2,1,0:T(8,128)(2,1)} %param.9) | copy-start | bytes 786436
  63.3 0.8 copy-start.6
  77.5 56.2 %all-to-all-start.1 = ((bf16[4,4,192,384]{3,2,0,1:T(8,128)(2,1)}), bf16[4,4,192,384]{3,2,0,1:T(8,128)(2,1)}, u32[]{:S(2)}, u32[]{:S(2)}) async-start(bf16[4,4,192,384]{3,2,0,1:T(8,128)(2,1)} %copy.72), calls=%async_computation.1 | async-start | bytes 4718592 | tf_op jit(solution)/shard_map/all_to_all | solution.py:132
  82.6 53.0 %copy-start.11 = (bf16[4,4,192]{2,1,0:T(4,128)(2,1)}, bf16[4,4,192]{2,1,0:T(4,128)(2,1)S(1)}, u32[]{:S(2)}) copy-start(bf16[4,4,192]{2,1,0:T(4,128)(2,1)S(1)} %copy.68) | copy-start | bytes 18436
  161.4 66.2 %all-to-all-start.2 = ((bf16[4,4,192,128]{3,2,0,1:T(8,128)(2,1)}), bf16[4,4,192,128]{3,2,0,1:T(8,128)(2,1)}, u32[]{:S(2)}, u32[]{:S(2)}) async-start(bf16[4,4,192,128]{3,2,0,1:T(8,128)(2,1)} %copy.76), calls=%async_computation.2 | async-start | bytes 1572864 | tf_op jit(solution)/shard_map/all_to_all | solution.py:141
  173.3 3.0 copy-start.9
  191.7 3.0 copy-start.9
  210.7 3.0 copy-start.9
  223.0 1.4 copy-start.8
  227.6 5.2 %copy-start.12 = (s32[1,4,256]{2,1,0:T(4,128)S(1)}, s32[1,4,256]{2,1,0:T(4,128)}, u32[]{:S(2)}) copy-start(s32[1,4,256]{2,1,0:T(4,128)} %param.12) | copy-start | bytes 12292
  227.6 58.0 %all-to-all-start.4 = ((bf16[4,4,192,384]{3,2,0,1:T(8,128)(2,1)}), bf16[4,4,192,384]{3,2,0,1:T(8,128)(2,1)}, u32[]{:S(2)}, u32[]{:S(2)}) async-start(bf16[4,4,192,384]{3,2,0,1:T(8,128)(2,1)} %copy.84), calls=%async_computation.5 | async-start | bytes 4718592 | tf_op jit(solution)/shard_map/all_to_all | solution.py:157
  232.8 8.0 %copy-start.2 = (bf16[1,256,1024]{2,1,0:T(8,128)(2,1)S(1)}, bf16[1,256,1024]{2,1,0:T(8,128)(2,1)}, u32[]{:S(2)}) copy-start(bf16[1,256,1024]{2,1,0:T(8,128)(2,1)} %copy-done.1) | copy-start | bytes 1572868
  232.8 172.4 %all-reduce.3.cloned.1.call-start = ((), (), s32[]{:S(2)}) async-start(), calls=%async_computation.9 | async-start | bytes 8388608 | tf_op jit(solution)/shard_map/psum | solution.py:169
  240.2 0.7 copy-start.4
  299.2 2.5 copy-start.7
  309.1 0.9 copy-start.5
  309.1 102.7 %reduce-scatter.3.cloned.1.call-start = ((), (), s32[]{:S(2)}) async-start(), calls=%async_computation.7 | async-start | bytes 786432 | tf_op jit(solution)/shard_map/reduce_scatter | solution.py:161
  311.3 100.5 %reduce-scatter.5.cloned.1.call-start = ((), (), s32[]{:S(2)}) async-start(), calls=%async_computation.8 | async-start | bytes 786432 | tf_op jit(solution)/shard_map/reduce_scatter | solution.py:173
  405.2 2.9 copy-start.3
Sparse Core Ops, SparseCore 0:
  309.2 95.9 all-reduce.2
Sparse Core Ops, SparseCore 1:
  312.4 13.6 reduce-scatter.2
  328.8 14.5 reduce-scatter.4
where the time goes:
time: 421 us; the launch traced here: 419 us
  waiting for transfers between devices  182 us (43%)
  matrix products  80 us (19%)
  local copies, waits for them, and re-layouts  74.3 us (18%)
  starting transfers between devices  25.7 us (6%)
  other arithmetic  21.4 us (5%)
  between operations  15.8 us (4%)
  blocking collectives  15.7 us (4%)
    psum x1, waiting for transfers between devices, shards(): lax.psum(grad_w_qkv_local.astype(jnp.bfloat16), ('ctx', 'dp'))  90.2 us
    all_to_all x1, waiting for transfers between devices, shards(): lax.all_to_all(pack(qkv_heads), 'ctx', split_axis=1, concat_axis=1, tiled...  48.7 us
    all_to_all x1, waiting for transfers between devices, shards(): lax.all_to_all(grads_own, 'ctx', split_axis=1, concat_axis=1, tiled=True)  43.4 us
    dot_general x8, matrix products, contract_first(): lax.dot_general(left, right, (((0,), (0,)), ((), ())), preferred_element_...  27.5 us
    unnamed x32, local copies, waits for them, and re-layouts  26.9 us
    sub x6, matrix products, masked_probs(): expo = jnp.exp(scores - top_value)  19.8 us
    gather x5, local copies, waits for them, and re-layouts, unpack(): jnp.take(table, where_to, axis=0)  19.6 us
    dot_general x5, matrix products, contract_last(): lax.dot_general(left, right, (((1,), (1,)), ((), ())), preferred_element_...  13.2 us
  transfers between devices with their start and end apart: 8, of which 3 were waited for; matrix products, arithmetic and copies ran while one was open for 25% of the time, Pallas kernels for 0%

commit v1 on v0

v1 whole, which is shorter than its diff:
```python
import functools

import jax
import jax.numpy as jnp
from jax import lax
from jax.experimental import pallas as pl
from jax.experimental.pallas import tpu as pltpu
from jax.sharding import PartitionSpec as P

HD = 128
F32 = jnp.float32
BF16 = jnp.bfloat16


def dot_general(left, right, left_dim, right_dim):
    return lax.dot_general(
        left, right, (((left_dim,), (right_dim,)), ((), ())), preferred_element_type=F32
    )


def project_kernel(rows_ref, grads_ref, w_qkv_ref, w_out_ref, out_ref):
    heads = out_ref.shape[0]
    size = heads * HD
    for j in range(3):
        part = dot_general(rows_ref[...], w_qkv_ref[:, j * size : (j + 1) * size], 1, 0).astype(BF16)
        for h in range(heads):
            out_ref[h, :, j * HD : (j + 1) * HD] = part[:, h * HD : (h + 1) * HD]
    part = dot_general(grads_ref[...], w_out_ref[...], 1, 1).astype(BF16)
    for h in range(heads):
        out_ref[h, :, 3 * HD :] = part[:, h * HD : (h + 1) * HD]


def attention_kernel(own_keys, block_rows, x_ref, kv_ref, mark_ref, key_mark_ref, *outs):
    if own_keys:
        (y_ref, gk_acc, gv_acc) = outs
        keys = x_ref[:, HD : 2 * HD]
        values = x_ref[:, 2 * HD : 3 * HD]
    else:
        (y_ref, gkv_ref, gk_acc, gv_acc) = outs
        keys = kv_ref[:, :HD]
        values = kv_ref[:, HD:]
    key_marks = key_mark_ref[...]
    count = x_ref.shape[0] // block_rows

    def one_block(b):
        rows = pl.ds(pl.multiple_of(b * block_rows, block_rows), block_rows)
        query = x_ref[rows, :HD]
        cot = x_ref[rows, 3 * HD :]
        scores = dot_general(query, keys, 1, 1) * HD ** (-0.5)
        scores = jnp.where(mark_ref[rows, :] == key_marks, scores, F32(-1e30))
        top = jnp.max(scores, axis=1, keepdims=True)
        expo = jnp.exp(scores - top)
        full = expo * (1.0 / jnp.sum(expo, axis=1, keepdims=True))
        probs = full.astype(BF16)
        attention = dot_general(probs, values, 1, 0).astype(BF16)
        dprob = dot_general(cot, values, 1, 1)
        delta = jnp.sum(cot.astype(F32) * attention.astype(F32), axis=1, keepdims=True)
        dscore = (full * (dprob - delta) * HD ** (-0.5)).astype(BF16)
        y_ref[rows, :HD] = dot_general(dscore, keys, 1, 0).astype(BF16)
        y_ref[rows, 3 * HD :] = attention
        return dot_general(dscore, query, 0, 0), dot_general(probs, cot, 0, 0)

    if count <= 4:
        grad_keys, grad_values = one_block(0)
        for b in range(1, count):
            more_keys, more_values = one_block(b)
            grad_keys = grad_keys + more_keys
            grad_values = grad_values + more_values
    else:
        gk_acc[...] = jnp.zeros_like(gk_acc)
        gv_acc[...] = jnp.zeros_like(gv_acc)

        @pl.loop(0, count)
        def _(b):
            more_keys, more_values = one_block(b)
            gk_acc[...] += more_keys
            gv_acc[...] += more_values

        grad_keys, grad_values = gk_acc[...], gv_acc[...]
    if own_keys:
        y_ref[:, HD : 2 * HD] = grad_keys.astype(BF16)
        y_ref[:, 2 * HD : 3 * HD] = grad_values.astype(BF16)
    else:
        gkv_ref[:, :HD] = grad_keys.astype(BF16)
        gkv_ref[:, HD:] = grad_values.astype(BF16)


def finish_kernel(z_ref, rows_ref, grads_ref, w_qkv_ref, w_out_ref, out_ref, in_ref, gwq_ref, gwo_ref):
    heads = z_ref.shape[0]
    size = heads * HD
    attention = jnp.concatenate([z_ref[h, :, 3 * HD :] for h in range(heads)], axis=1)
    out_ref[...] = dot_general(attention, w_out_ref[...], 1, 0).astype(BF16)
    gwo_ref[...] = dot_general(attention, grads_ref[...], 0, 0).astype(BF16)
    total = None
    for j in range(3):
        grad = jnp.concatenate([z_ref[h, :, j * HD : (j + 1) * HD] for h in range(heads)], axis=1)
        cols = slice(j * size, (j + 1) * size)
        term = dot_general(grad, w_qkv_ref[:, cols], 1, 1)
        total = term if total is None else total + term
        gwq_ref[:, cols] = dot_general(rows_ref[...], grad, 0, 0).astype(BF16)
    in_ref[...] = total.astype(BF16)


VMEM_SPEC = pl.BlockSpec(memory_space=pltpu.VMEM)


def call(kernel, shapes, scratch=(), **kw):
    return pl.pallas_call(
        kernel,
        out_shape=[jax.ShapeDtypeStruct(s, t) for s, t in shapes],
        out_specs=[VMEM_SPEC] * len(shapes),
        scratch_shapes=list(scratch),
        compiler_params=pltpu.CompilerParams(vmem_limit_bytes=56 * 2**20),
        **kw,
    )


def shards(tokens, w_qkv, w_out, labels, grad_out):
    heads = w_out.shape[0] // HD
    ctx_count = lax.axis_size("ctx")
    repeat = ctx_count // heads
    inner = [[g * heads + i for i in range(heads)] for g in range(repeat)]
    outer = [[g * heads + i for g in range(repeat)] for i in range(heads)]
    width = w_qkv.shape[0]
    size = heads * HD
    w_flat = w_qkv.reshape(width, 3 * size)

    marks_all = lax.all_gather(labels[0], "ctx", axis=1, tiled=True)
    rows = lax.all_gather(tokens, "tensor", axis=2, tiled=True)[0]
    grads = lax.all_gather(grad_out, "tensor", axis=2, tiled=True)[0]
    count = rows.shape[0]

    (packed,) = call(project_kernel, [((heads, count, 4 * HD), BF16)], in_specs=[VMEM_SPEC] * 4)(
        rows, grads, w_flat, w_out
    )
    me = lax.axis_index("ctx")
    head_of = me % heads
    exchange = functools.partial(
        lax.all_to_all, axis_name="ctx", split_axis=0, concat_axis=0, tiled=True, axis_index_groups=inner
    )
    mine = exchange(packed).reshape(heads * count, 4 * HD)
    total = heads * count
    key_marks = lax.dynamic_slice_in_dim(marks_all, head_of, 1, 0)
    row_marks = lax.dynamic_slice_in_dim(key_marks, (me // heads) * total, total, 1).reshape(total, 1)
    key_total = total * repeat
    block_rows = 256
    acc = [pltpu.VMEM((key_total, HD), F32)] * 2 if total // block_rows > 4 else [pltpu.VMEM((8, HD), F32)] * 2
    if repeat == 1:
        (back,) = call(
            functools.partial(attention_kernel, True, block_rows),
            [((total, 4 * HD), BF16)],
            acc,
            in_specs=[VMEM_SPEC] * 4,
        )(mine, mine[:8, : 2 * HD], row_marks, key_marks)
    else:
        keys_values = lax.all_gather(
            mine[:, HD : 3 * HD], "ctx", axis=0, tiled=True, axis_index_groups=outer
        )
        back, terms = call(
            functools.partial(attention_kernel, False, block_rows),
            [((total, 4 * HD), BF16), ((key_total, 2 * HD), BF16)],
            acc,
            in_specs=[VMEM_SPEC] * 4,
        )(mine, keys_values, row_marks, key_marks)
        summed = lax.psum_scatter(
            terms, "ctx", scatter_dimension=0, tiled=True, axis_index_groups=outer
        )
        back = jnp.concatenate([back[:, :HD], summed, back[:, 3 * HD :]], axis=1)
    home = exchange(back.reshape(heads, count, 4 * HD))
    out_terms, in_terms, grad_w_qkv, grad_w_out = call(
        finish_kernel,
        [
            ((count, width), BF16),
            ((count, width), BF16),
            ((width, 3 * size), BF16),
            ((size, width), BF16),
        ],
        in_specs=[VMEM_SPEC] * 5,
    )(home, rows, grads, w_flat, w_out)
    summed_qkv = lax.psum(grad_w_qkv, ("ctx", "dp")).astype(F32).reshape(width, 3, size)
    summed_out = lax.psum(grad_w_out, ("ctx", "dp")).astype(F32)
    attended = lax.psum_scatter(out_terms, "tensor", scatter_dimension=1, tiled=True)
    grad_tokens = lax.psum_scatter(in_terms, "tensor", scatter_dimension=1, tiled=True)
    return (attended[None], grad_tokens[None], summed_qkv, summed_out)


def solution(mesh):
    placed = (
        P(("groups", "dp"), "ctx", "tensor"),
        P(None, None, "tensor"),
        P("tensor", None),
        P(("groups", "dp"), "tensor", "ctx"),
        P(("groups", "dp"), "ctx", "tensor"),
    )
    return jax.shard_map(
        shards,
        mesh=mesh,
        in_specs=placed,
        out_specs=(
            P(("groups", "dp"), "ctx", "tensor"),
            P(("groups", "dp"), "ctx", "tensor"),
            P("groups", None, "tensor"),
            P(("groups", "tensor"), None),
        ),
        check_vma=False,
    )
```

time: 421 us -> 234 us (0.56)
  waiting for transfers between devices: 182 us -> 96.1 us
  matrix products: 80 us -> 0 us
  blocking collectives: 15.7 us -> 77 us
  local copies, waits for them, and re-layouts: 74.3 us -> 18.8 us
  starting transfers between devices: 25.7 us -> 5.37 us
  other arithmetic: 21.4 us -> 1.57 us
  Pallas kernels: 0 us -> 18.9 us
    all_to_all x5 -> x1, waiting for transfers between devices: 92.2 us -> 0.01 us  [shards(): mine = exchange(packed).reshape(heads * count, 4 * HD)]
    dot_general x21 -> x0, matrix products: 60.2 us -> none  [the longest x8 27.5 us: contract_first(): lax.dot_general(left, right, (((0,), (0,)), ((), ())), preferred_element_...]
    all_gather x2 -> x3, blocking collectives: 15.7 us -> 50.4 us  [the longest x1 30 us: shards(): marks_all = lax.all_gather(labels[0], 'ctx', axis=1, tiled=True)]
    all_to_all x0 -> x1, blocking collectives: none -> 26.7 us  [shards(): home = exchange(back.reshape(heads, count, 4 * HD))]
    all_to_all x5 -> x1, starting transfers between devices: 25.6 us -> 5.28 us  [shards(): mine = exchange(packed).reshape(heads * count, 4 * HD)]
    sub x6 -> x0, matrix products: 19.8 us -> none  [masked_probs(): expo = jnp.exp(scores - top_value)]
    gather x5 -> x0, local copies, waits for them, and re-layouts: 19.6 us -> none  [unpack(): jnp.take(table, where_to, axis=0)]
    pallas_call x0 -> x3, Pallas kernels: none -> 18.9 us  [the longest x1 7.37 us: shards(): call(functools.partial(attention_kernel, True, block_rows), [((total, 4 *...]
  transfers between devices with their start and end apart: 8 -> 4, of which waited for: 3 -> 1; matrix products, arithmetic and copies ran while one was open for 25% -> 4% of each run, Pallas kernels for 0% -> 0%
where the time goes in v1:
time: 234 us; the launch traced here: 233 us
  waiting for transfers between devices  96.1 us (41%)
  blocking collectives  77 us (33%)
  Pallas kernels  18.9 us (8%)
  local copies, waits for them, and re-layouts  18.8 us (8%)
  between operations  15.5 us (7%)
  starting transfers between devices  5.37 us (2%)
    psum x1, waiting for transfers between devices, shards(): lax.psum(grad_w_qkv, ('ctx', 'dp')).astype(F32).reshape(width, 3, size)  95 us
    all_gather x1, blocking collectives, shards(): marks_all = lax.all_gather(labels[0], 'ctx', axis=1, tiled=True)  30 us
    all_to_all x1, blocking collectives, shards(): home = exchange(back.reshape(heads, count, 4 * HD))  26.7 us
    all_gather x1, blocking collectives, shards(): rows = lax.all_gather(tokens, 'tensor', axis=2, tiled=True)[0]  11.9 us
    unnamed x8, local copies, waits for them, and re-layouts  9 us
    all_gather x1, blocking collectives, shards(): grads = lax.all_gather(grad_out, 'tensor', axis=2, tiled=True)[0]  8.47 us
    pallas_call x1, Pallas kernels, shards(): call(functools.partial(attention_kernel, True, block_rows), [((total, 4 *...  7.37 us
    pallas_call x1, Pallas kernels, shards(): call(finish_kernel, [((count, width), BF16), ((count, width), BF16), ((wi...  6.8 us
  transfers between devices with their start and end apart: 4, of which 1 were waited for; matrix products, arithmetic and copies ran while one was open for 4% of the time, Pallas kernels for 0%

profile of v1, /device:TPU:0, one launch (start us, length us, event | category | flops | bytes accessed | tf_op | source)
XLA Modules:
  0.0 233.3 jit_solution(13736699656799751153)
XLA Ops:
  8.0 11.9 %all_gather.9 = bf16[1,256,1024]{2,1,0:T(8,128)(2,1)} all-gather(bf16[1,256,512]{2,1,0:T(8,128)(2,1)} %param.5), channel_id=1, replica_groups=mesh['groups'=2,'ctx'=4,'tensor'=2,'dp'=2] {'tensor'}, dimensions={2}, use_global_device_ids=true | all-gather | bytes 786432 | tf_op jit(solution)/shard_map/all_gather | solution.py:129
  19.9 8.5 %all_gather.10 = bf16[1,256,1024]{2,1,0:T(8,128)(2,1)} all-gather(bf16[1,256,512]{2,1,0:T(8,128)(2,1)} %param.9), channel_id=1, replica_groups=mesh['groups'=2,'ctx'=4,'tensor'=2,'dp'=2] {'tensor'}, dimensions={2}, use_global_device_ids=true | all-gather | bytes 786432 | tf_op jit(solution)/shard_map/all_gather | solution.py:130
  28.4 3.2 %copy.11 = bf16[1024,3,512]{0,2,1:T(8,128)(2,1)S(1)} copy(bf16[1024,3,512]{2,0,1:T(8,128)(2,1)} %param.6) | data formatting | bytes 6291456 | tf_op args[1]
  31.6 2.9 %copy.12.w_qkv_ref = bf16[1024,1536]{1,0:T(8,128)(2,1)} copy(bf16[1024,1536]{0,1:T(8,128)(2,1)S(1)} %bitcast.13) | data formatting | bytes 6291456 | tf_op jit(solution)/shard_map/reshape | solution.py:126
  34.5 4.7 %shard_map.84 = bf16[4,256,512]{2,1,0:T(8,128)(2,1)} custom-call(bf16[256,1024]{1,0:T(8,128)(2,1)} %bitcast.14, bf16[256,1024]{1,0:T(8,128)(2,1)} %bitcast.16, bf16[1024,1536]{1,0:T(8,128)(2,1)} %copy.12.w_qkv_ref, bf16[512,1024]{1,0:T(8,128)(2,1)} %w_out_ref.3), custom_call_target="tpu_custom_call" | custom-call | tf_op jit(solution)/shard_map/pallas_call | solution.py:133
  39.2 5.3 %all-to-all-start = ((bf16[4,256,512]{2,1,0:T(8,128)(2,1)}), bf16[4,256,512]{2,1,0:T(8,128)(2,1)S(1)}, u32[]{:S(2)}, u32[]{:S(2)}) async-start(bf16[4,256,512]{2,1,0:T(8,128)(2,1)} %shard_map.84), calls=%async_computation | async-start | bytes 2097152 | tf_op jit(solution)/shard_map/all_to_all | solution.py:141
  44.5 30.0 %all-gather = s32[1,4,1024]{2,1,0:T(4,128)S(1)} all-gather(s32[1,4,256]{2,1,0:T(4,128)S(1)} %copy-done.2), channel_id=2, replica_groups=mesh['groups'=2,'ctx'=4,'tensor'=2,'dp'=2] {'ctx'}, dimensions={2}, use_global_device_ids=true | all-gather | bytes 20480 | tf_op jit(solution)/shard_map/all_gather | solution.py:128
  74.5 0.6 dynamic-slice_bitcast_fusion.1
  75.1 1.1 copy.13.mark_ref
  76.1 0.0 all-to-all-done
  76.1 0.6 slice.4.kv_ref
  76.8 0.3 copy-done
  77.1 7.4 %shard_map.85 = bf16[1024,512]{1,0:T(8,128)(2,1)} custom-call(bf16[1024,512]{1,0:T(8,128)(2,1)} %bitcast.19, bf16[8,256]{1,0:T(8,128)(2,1)} %slice.4.kv_ref, s32[1024,1]{1,0:T(8,128)} %copy.13.mark_ref, s32[1,1024]{1,0:T(1,128)} %get-tuple-element.18.key_mark_ref), custom_call_target="tpu_custom_call" | custom-call | tf_op jit(solution)/shard_map/pallas_call | solution.py:149
  84.5 26.7 %all_to_all.10.z_ref = bf16[4,256,512]{2,1,0:T(8,128)(2,1)} all-to-all(bf16[4,256,512]{2,1,0:T(8,128)(2,1)} %bitcast.20), channel_id=1, replica_groups={{0,4,8,12},{1,5,9,13},{2,6,10,14},{3,7,11,15},{16,20,24,28},{17,21,25,2..., dimensions={0} | all-to-all | bytes 2097152 | tf_op jit(solution)/shard_map/all_to_all | solution.py:169
  111.2 6.8 %shard_map.86 = (bf16[256,1024]{1,0:T(8,128)(2,1)}, bf16[256,1024]{1,0:T(8,128)(2,1)}, bf16[1024,1536]{1,0:T(8,128)(2,1)}, bf16[512,1024]{1,0:T(8,128)(2,1)}) custom-call(bf16[4,256,512]{2,1,0:T(8,128)(2,1)} %all_to_all.10.z_ref, bf16[256,1024]{1,0:T(8,128)(2,1)} %bitcast.15, bf16[256,1024]{1,0:T(8,128)(2,1)} %bitcast.17, ...), custom_call_target="tpu_custom_call" | custom-call | tf_op jit(solution)/shard_map/pallas_call | solution.py:170
  118.0 4.6 %copy.15 = bf16[1024,1536]{0,1:T(8,128)(2,1)} copy(bf16[1024,1536]{1,0:T(8,128)(2,1)} %get-tuple-element.10) | data formatting | bytes 6291456 | tf_op jit(solution)/shard_map/pallas_call | solution.py:170
  122.6 0.0 all-reduce.3.cloned.1.call-update
  122.6 0.0 reduce-scatter.3.cloned.1.call-start
  122.7 0.5 reduce-scatter.3.cloned.1.call-update
  123.2 0.0 reduce-scatter.5.cloned.1.call-start
  123.3 0.5 reduce-scatter.5.cloned.1.call-update
  123.8 95.0 %all-reduce.3.cloned.1.call-done = (bf16[1024,3,512]{0,2,1:T(8,128)(2,1)}, bf16[512,1024]{1,0:T(8,128)(2,1)}) async-done(((bf16[1024,3,512]{0,2,1:T(8,128)(2,1)}, bf16[512,1024]{1,0:T(8,128)(2,1)}), (bf16[1024,3,512]{0,2,1:T(8,128)(2,1)}, bf16[512,1024]{1,0:T(8,128)(2,1)})) %all-reduce.3.cloned.1.call-update) | async-done | bytes 4194320 | tf_op jit(solution)/shard_map/psum | solution.py:180
  218.9 5.5 %copy.16 = f32[1024,3,512]{2,0,1:T(8,128)} copy(bf16[1024,3,512]{0,2,1:T(8,128)(2,1)} %get-tuple-element.16) | data formatting | bytes 9437184
  224.3 1.6 convert_element_type.4
  (8 shorter events, 0.0 us)
Async XLA Ops:
  34.5 10.0 %copy-start.2 = (s32[1,4,256]{2,1,0:T(4,128)S(1)}, s32[1,4,256]{2,1,0:T(4,128)}, u32[]{:S(2)}) copy-start(s32[1,4,256]{2,1,0:T(4,128)} %param.8) | copy-start | bytes 12292
  39.2 36.9 %all-to-all-start = ((bf16[4,256,512]{2,1,0:T(8,128)(2,1)}), bf16[4,256,512]{2,1,0:T(8,128)(2,1)S(1)}, u32[]{:S(2)}, u32[]{:S(2)}) async-start(bf16[4,256,512]{2,1,0:T(8,128)(2,1)} %shard_map.84), calls=%async_computation | async-start | bytes 2097152 | tf_op jit(solution)/shard_map/all_to_all | solution.py:141
  44.5 174.3 %all-reduce.3.cloned.1.call-start = ((), (), s32[]{:S(2)}) async-start(), calls=%async_computation.6 | async-start | bytes 8388608 | tf_op jit(solution)/shard_map/psum | solution.py:180
  76.1 1.0 copy-start
  122.6 103.3 %reduce-scatter.3.cloned.1.call-start = ((), (), s32[]{:S(2)}) async-start(), calls=%async_computation.4 | async-start | bytes 786432 | tf_op jit(solution)/shard_map/reduce_scatter | solution.py:182
  123.2 102.7 %reduce-scatter.5.cloned.1.call-start = ((), (), s32[]{:S(2)}) async-start(), calls=%async_computation.5 | async-start | bytes 786432 | tf_op jit(solution)/shard_map/reduce_scatter | solution.py:183
  218.9 5.5 %copy-start.1 = (bf16[512,1024]{1,0:T(8,128)(2,1)S(1)}, bf16[512,1024]{1,0:T(8,128)(2,1)}, u32[]{:S(2)}) copy-start(bf16[512,1024]{1,0:T(8,128)(2,1)} %get-tuple-element.17) | copy-start | bytes 3145732
Sparse Core Ops, SparseCore 0:
  122.8 96.0 all-reduce.2
Sparse Core Ops, SparseCore 1:
  125.9 13.6 reduce-scatter.2
  142.4 14.5 reduce-scatter.4

commit v2 on v1

--- a/solution.py
+++ b/solution.py
@@ -101,6 +101,387 @@
     in_ref[...] = total.astype(BF16)
 
 
+def remote(source, target, send_sem, recv_sem, device):
+    return pltpu.make_async_remote_copy(
+        src_ref=source,
+        dst_ref=target,
+        send_sem=send_sem,
+        recv_sem=recv_sem,
+        device_id=device,
+        device_id_type=pl.DeviceIdType.MESH,
+    )
+
+
+def layer_kernel(
+    tok_ref, gro_ref, w3_ref, wo_ref, lab_ref,
+    att_out, tokgrad_out, res_out,
+    rows, grads, acc, packed, heads_in, marks, full, y, home,
+    part, from_core, chip_sum, from_outer, from_inner, res, x_send, x_recv, x_own, tok_out,
+    sx, rx, sl, rl, sa, ra, sb, rb, su, ru, so, ro, si, ri, sq, rq, sp, rp, sc, rc, st, rt, lsem,
+):
+    z = lax.axis_index("ctx")
+    x = lax.axis_index("tensor")
+    c = lax.axis_index("dp")
+    count = tok_ref.shape[0]
+    half = tok_ref.shape[1]
+    scale = HD ** (-0.5)
+    other_x = 1 - x
+    other_c = 1 - c
+    x_dev = {"tensor": other_x}
+    c_dev = {"dp": other_c}
+    peers = [lax.rem(z + d, 4) for d in range(1, 4)]
+    sources = [lax.rem(z + 4 - d, 4) for d in range(1, 4)]
+
+    barrier = pltpu.get_barrier_semaphore()
+    for device in [{"ctx": p} for p in peers] + [x_dev, c_dev]:
+        pl.semaphore_signal(barrier, inc=1, device_id=device, device_id_type=pl.DeviceIdType.MESH)
+    pl.semaphore_wait(barrier, 5)
+
+    def block(index, size):
+        return pl.ds(pl.multiple_of(index * size, size), size)
+
+    x_copies = [
+        remote(tok_ref, rows.at[x], sx.at[0], rx.at[0], x_dev),
+        remote(gro_ref, grads.at[x], sx.at[1], rx.at[1], x_dev),
+    ]
+    for copy in x_copies:
+        copy.start()
+    label_copies = []
+    for d in range(3):
+        label_copies.append(
+            remote(lab_ref.at[peers[d]], marks.at[z], sl.at[d], rl.at[d], {"ctx": peers[d]})
+        )
+        label_copies[-1].start()
+    rows[x] = tok_ref[...]
+    grads[x] = gro_ref[...]
+    marks[z] = lab_ref[z]
+    for j in range(3):
+        acc[j] = dot_general(tok_ref[...], w3_ref[j, block(x, half), :], 1, 0)
+    acc[3] = dot_general(gro_ref[...], wo_ref[:, block(x, half)], 1, 1)
+
+    a_copies = []
+    for j in range(4):
+        if j == 0:
+            x_copies[0].wait_recv()
+        if j == 3:
+            x_copies[1].wait_recv()
+        if j < 3:
+            term = dot_general(rows[other_x], w3_ref[j, block(other_x, half), :], 1, 0)
+        else:
+            term = dot_general(grads[other_x], wo_ref[:, block(other_x, half)], 1, 1)
+        value = (acc[j] + term).astype(BF16)
+        for h in range(4):
+            packed[j, h] = value[:, h * HD : (h + 1) * HD]
+        for d in range(3):
+            copy = remote(
+                packed.at[j, peers[d]],
+                heads_in.at[j, block(z, count), :],
+                sa.at[j, d],
+                ra.at[j, d],
+                {"ctx": peers[d]},
+            )
+            copy.start()
+            a_copies.append(copy)
+        heads_in[j, block(z, count), :] = packed[j, z]
+
+    for copy in label_copies:
+        copy.wait_recv()
+    for copy in a_copies[:9]:
+        copy.wait_recv()
+    keys = heads_in[1]
+    values = heads_in[2]
+    key_marks = jnp.concatenate([marks[s].astype(F32) for s in range(4)], axis=1)
+    order = [*peers, z]
+    b_copies = []
+
+    def send_back(j, d):
+        copy = remote(
+            y.at[j, block(order[d], count), :],
+            home.at[j, z],
+            sb.at[j, d],
+            rb.at[j, d],
+            {"ctx": order[d]},
+        )
+        copy.start()
+        b_copies.append(copy)
+
+    for d in range(4):
+        here = block(order[d], count)
+        mine = jnp.broadcast_to(marks[order[d]].astype(F32), (HD, count)).T[:, :1]
+        scores = dot_general(heads_in[0, here, :], keys, 1, 1) * scale
+        scores = jnp.where(mine == key_marks, scores, F32(-1e30))
+        expo = jnp.exp(scores - jnp.max(scores, axis=1, keepdims=True))
+        probs_full = expo * (1.0 / jnp.sum(expo, axis=1, keepdims=True))
+        full[d] = probs_full
+        y[3, here, :] = dot_general(probs_full.astype(BF16), values, 1, 0).astype(BF16)
+        if d < 3:
+            send_back(3, d)
+    home[3, z] = y[3, block(z, count), :]
+    for copy in a_copies[9:]:
+        copy.wait_recv()
+    grad_keys = grad_values = None
+    for d in range(4):
+        here = block(order[d], count)
+        cot = heads_in[3, here, :]
+        probs_full = full[d]
+        dprob = dot_general(cot, values, 1, 1)
+        delta = jnp.sum(cot.astype(F32) * y[3, here, :].astype(F32), axis=1, keepdims=True)
+        dscore = (probs_full * (dprob - delta) * scale).astype(BF16)
+        y[0, here, :] = dot_general(dscore, keys, 1, 0).astype(BF16)
+        if d < 3:
+            send_back(0, d)
+        more_keys = dot_general(dscore, heads_in[0, here, :], 0, 0)
+        more_values = dot_general(probs_full.astype(BF16), cot, 0, 0)
+        grad_keys = more_keys if d == 0 else grad_keys + more_keys
+        grad_values = more_values if d == 0 else grad_values + more_values
+    home[0, z] = y[0, block(z, count), :]
+    y[1] = grad_keys.astype(BF16)
+    for d in range(3):
+        send_back(1, d)
+    home[1, z] = y[1, block(z, count), :]
+    y[2] = grad_values.astype(BF16)
+    for d in range(3):
+        send_back(2, d)
+    home[2, z] = y[2, block(z, count), :]
+
+    b_at = {3: b_copies[0:3], 0: b_copies[3:6], 1: b_copies[6:9], 2: b_copies[9:12]}
+    units = (3, 0, 1, 2)
+    u_copies = {}
+    kept = {}
+
+    def unit_term(u, grad, f):
+        if u == 3:
+            return dot_general(grad, grads[f], 0, 0)
+        return dot_general(rows[f], grad, 0, 0)
+
+    for u in units:
+        for copy in b_at[u]:
+            copy.wait_recv()
+        grad = jnp.concatenate([home[u, h] for h in range(4)], axis=1)
+        part[u] = unit_term(u, grad, other_c).astype(BF16)
+        u_copies[u] = remote(part.at[u], from_core.at[u], su.at[u], ru.at[u], c_dev)
+        u_copies[u].start()
+        chip_sum[u] = unit_term(u, grad, c).astype(BF16)
+
+    inner = jnp.logical_or(z == 1, z == 2)
+    side = z // 2
+    inner_of_outer = jnp.where(z == 0, 1, 2)
+    outer_dev = {"ctx": jnp.where(z == 1, 0, 3)}
+    inner_dev = {"ctx": jnp.where(z == 1, 2, 1)}
+    steps = [(u, k) for u in units for k in range(2)]
+
+    def chunk(which, k):
+        return pl.ds(pl.multiple_of(which * 256 + k * 128, 128), 128)
+
+    def outer_send(n, which):
+        u, k = steps[n]
+        at = chunk(which, k)
+        q = n * 2 + which
+        return remote(
+            chip_sum.at[u, at, :], from_outer.at[u, at, :], so.at[q], ro.at[q], {"ctx": inner_of_outer}
+        )
+
+    def from_outer_copy(n, which):
+        u, k = steps[n]
+        at = chunk(which, k)
+        q = n * 2 + which
+        return remote(chip_sum.at[u, at, :], from_outer.at[u, at, :], so.at[q], ro.at[q], outer_dev)
+
+    def inner_partial(n, which):
+        u, k = steps[n]
+        at = chunk(which, k)
+        return remote(chip_sum.at[u, at, :], from_inner.at[u, at, :], si.at[n], ri.at[n], inner_dev)
+
+    def inner_result(n, which):
+        u, k = steps[n]
+        at = chunk(which, k)
+        return remote(res.at[u, c, at, :], res.at[u, c, at, :], sq.at[n], rq.at[n], inner_dev)
+
+    def outer_result(n, which, device):
+        u, k = steps[n]
+        at = chunk(which, k)
+        q = n * 2 + which
+        return remote(res.at[u, c, at, :], res.at[u, c, at, :], sp.at[q], rp.at[q], device)
+
+    def core_result(n, which):
+        u, k = steps[n]
+        at = chunk(which, k)
+        q = n * 2 + which
+        return remote(res.at[u, c, at, :], res.at[u, c, at, :], sc.at[q], rc.at[q], c_dev)
+
+    def core_result_in(n, which):
+        u, k = steps[n]
+        at = chunk(which, k)
+        q = n * 2 + which
+        return remote(res.at[u, other_c, at, :], res.at[u, other_c, at, :], sc.at[q], rc.at[q], c_dev)
+
+    near, far = side, 1 - side
+    for u in units:
+        u_copies[u].wait_recv()
+        chip_sum[u] = (chip_sum[u].astype(F32) + from_core[u].astype(F32)).astype(BF16)
+
+        @pl.when(jnp.logical_not(inner))
+        def _(u=u):
+            for k in range(2):
+                n = steps.index((u, k))
+                outer_send(n, far).start()
+                outer_send(n, near).start()
+
+    t_copies = []
+
+    def token_term(t, f):
+        if t == 0:
+            grad = jnp.concatenate([home[3, h] for h in range(4)], axis=1)
+            return dot_general(grad, wo_ref[:, block(f, half)], 1, 0)
+        total = None
+        for j in range(3):
+            grad = jnp.concatenate([home[j, h] for h in range(4)], axis=1)
+            term = dot_general(grad, w3_ref[j, block(f, half), :], 1, 1)
+            total = term if total is None else total + term
+        return total
+
+    for t in range(2):
+        x_send[t] = token_term(t, other_x).astype(BF16)
+        t_copies.append(remote(x_send.at[t], x_recv.at[t], st.at[t], rt.at[t], x_dev))
+        t_copies[t].start()
+    for t in range(2):
+        x_own[t] = token_term(t, x)
+
+    count_steps = len(steps)
+    lag = 2
+
+    @pl.when(inner)
+    def _():
+        def relay(n):
+            inner_result(n, far).wait_recv()
+            outer_result(n, far, outer_dev).start()
+            core_result(n, far).start()
+
+        for n in range(count_steps):
+            u, k = steps[n]
+            far_at, near_at = chunk(far, k), chunk(near, k)
+            from_outer_copy(n, far).wait_recv()
+            chip_sum[u, far_at, :] = (
+                chip_sum[u, far_at, :].astype(F32) + from_outer[u, far_at, :].astype(F32)
+            ).astype(BF16)
+            inner_partial(n, far).start()
+            from_outer_copy(n, near).wait_recv()
+            inner_partial(n, near).wait_recv()
+            res[u, c, near_at, :] = (
+                chip_sum[u, near_at, :].astype(F32)
+                + from_outer[u, near_at, :].astype(F32)
+                + from_inner[u, near_at, :].astype(F32)
+            ).astype(BF16)
+            inner_result(n, near).start()
+            outer_result(n, near, outer_dev).start()
+            core_result(n, near).start()
+            if n >= lag:
+                relay(n - lag)
+        for n in range(count_steps - lag, count_steps):
+            relay(n)
+        for n in range(count_steps):
+            inner_partial(n, far).wait_send()
+            inner_result(n, near).wait_send()
+            for which in (near, far):
+                outer_result(n, which, outer_dev).wait_send()
+
+    @pl.when(jnp.logical_not(inner))
+    def _():
+        back = {"ctx": inner_of_outer}
+        for n in range(count_steps):
+            outer_result(n, near, back).wait_recv()
+            core_result(n, near).start()
+            if n >= lag:
+                outer_result(n - lag, far, back).wait_recv()
+                core_result(n - lag, far).start()
+        for n in range(count_steps - lag, count_steps):
+            outer_result(n, far, back).wait_recv()
+            core_result(n, far).start()
+        for n in range(count_steps):
+            for which in (near, far):
+                outer_send(n, which).wait_send()
+
+    own_out = [
+        pltpu.make_async_copy(res.at[u, c], res_out.at[u, c], lsem.at[u]) for u in units
+    ]
+    for copy in own_out:
+        copy.start()
+    for t in range(2):
+        t_copies[t].wait_recv()
+        tok_out[t] = (x_own[t].astype(BF16).astype(F32) + x_recv[t].astype(F32)).astype(BF16)
+    token_out = [
+        pltpu.make_async_copy(tok_out.at[0], att_out, lsem.at[8]),
+        pltpu.make_async_copy(tok_out.at[1], tokgrad_out, lsem.at[9]),
+    ]
+    for copy in token_out:
+        copy.start()
+    other_out = []
+    for i, u in enumerate(units):
+        for n in (2 * i, 2 * i + 1):
+            for which in (near, far):
+                core_result_in(n, which).wait_recv()
+        copy = pltpu.make_async_copy(res.at[u, other_c], res_out.at[u, other_c], lsem.at[4 + u])
+        copy.start()
+        other_out.append(copy)
+    for copy in own_out + token_out + other_out:
+        copy.wait()
+    for copy in [*x_copies, *label_copies, *a_copies, *b_copies, *u_copies.values(), *t_copies]:
+        copy.wait_send()
+    for n in range(count_steps):
+        for which in (near, far):
+            core_result(n, which).wait_send()
+
+
+def whole_layer(tokens, w_qkv, w_out, labels, grad_out):
+    count, half = tokens.shape[1:]
+    width = w_qkv.shape[0]
+    size = w_out.shape[0]
+    any_spec = pl.BlockSpec(memory_space=pl.ANY)
+    dma = pltpu.SemaphoreType.DMA
+    square = (4, half, size)
+    scratch = [
+        pltpu.VMEM((2, count, half), BF16),
+        pltpu.VMEM((2, count, half), BF16),
+        pltpu.VMEM((4, count, size), F32),
+        pltpu.VMEM((4, 4, count, HD), BF16),
+        pltpu.VMEM((4, 4 * count, HD), BF16),
+        pltpu.VMEM((4, 1, count), jnp.int32),
+        pltpu.VMEM((4, count, 4 * count), F32),
+        pltpu.VMEM((4, 4 * count, HD), BF16),
+        pltpu.VMEM((4, 4, count, HD), BF16),
+        pltpu.VMEM(square, BF16),
+        pltpu.VMEM(square, BF16),
+        pltpu.VMEM(square, BF16),
+        pltpu.VMEM(square, BF16),
+        pltpu.VMEM(square, BF16),
+        pltpu.VMEM((4, 2, half, size), BF16),
+        pltpu.VMEM((2, count, half), BF16),
+        pltpu.VMEM((2, count, half), BF16),
+        pltpu.VMEM((2, count, half), F32),
+        pltpu.VMEM((2, count, half), BF16),
+    ]
+    for shape in ((2,), (3,), (4, 3), (4, 3), (4,), (16,), (8,), (8,), (16,), (16,), (2,)):
+        scratch += [dma(shape), dma(shape)]
+    scratch.append(dma((10,)))
+    attended, grad_tokens, sums = pl.pallas_call(
+        layer_kernel,
+        out_shape=[
+            jax.ShapeDtypeStruct((count, half), BF16),
+            jax.ShapeDtypeStruct((count, half), BF16),
+            jax.ShapeDtypeStruct((4, 2, half, size), BF16),
+        ],
+        in_specs=[VMEM_SPEC] * 5,
+        out_specs=[any_spec] * 3,
+        scratch_shapes=scratch,
+        compiler_params=pltpu.CompilerParams(
+            collective_id=0, has_side_effects=True, vmem_limit_bytes=56 * 2**20
+        ),
+    )(tokens[0], grad_out[0], jnp.transpose(w_qkv, (1, 0, 2)), w_out, labels[0][:, None, :])
+    grad_w_qkv = jnp.transpose(sums[:3].astype(F32).reshape(3, width, size), (1, 0, 2))
+    grad_w_out = jnp.transpose(sums[3].astype(F32), (1, 0, 2)).reshape(size, width)
+    return attended[None], grad_tokens[None], grad_w_qkv, grad_w_out
+
+
 VMEM_SPEC = pl.BlockSpec(memory_space=pltpu.VMEM)
 
 
@@ -118,6 +499,14 @@
 def shards(tokens, w_qkv, w_out, labels, grad_out):
     heads = w_out.shape[0] // HD
     ctx_count = lax.axis_size("ctx")
+    if (
+        ctx_count == 4
+        and heads == 4
+        and lax.axis_size("tensor") == 2
+        and lax.axis_size("dp") == 2
+        and tokens.shape[1:] == (256, 512)
+    ):
+        return whole_layer(tokens, w_qkv, w_out, labels, grad_out)
     repeat = ctx_count // heads
     inner = [[g * heads + i for i in range(heads)] for g in range(repeat)]
     outer = [[g * heads + i for g in range(repeat)] for i in range(heads)]

time: 234 us -> 152 us (0.65)
  Pallas kernels: 18.9 us -> 134 us
  waiting for transfers between devices: 96.1 us -> 0 us
  blocking collectives: 77 us -> 0 us
  between operations: 15.5 us -> 0.65 us
  local copies, waits for them, and re-layouts: 18.8 us -> 10.6 us
  starting transfers between devices: 5.37 us -> 0 us
  other arithmetic: 1.57 us -> 6.64 us
    pallas_call x3 -> x1, Pallas kernels: 18.9 us -> 134 us  [whole_layer(): pl.pallas_call(layer_kernel, out_shape=[jax.ShapeDtypeStruct((count, half...]
    psum x1 -> x0, waiting for transfers between devices: 95 us -> none  [shards(): lax.psum(grad_w_qkv, ('ctx', 'dp')).astype(F32).reshape(width, 3, size)]
    all_gather x3 -> x0, blocking collectives: 50.4 us -> none  [the longest x1 30 us: shards(): marks_all = lax.all_gather(labels[0], 'ctx', axis=1, tiled=True)]
    all_to_all x1 -> x0, blocking collectives: 26.7 us -> none  [shards(): home = exchange(back.reshape(heads, count, 4 * HD))]
    all_to_all x1 -> x0, starting transfers between devices: 5.28 us -> none  [shards(): mine = exchange(packed).reshape(heads * count, 4 * HD)]
    unnamed x8 -> x7, local copies, waits for them, and re-layouts: 9 us -> 4.29 us
    pallas_call x1 -> x0, local copies, waits for them, and re-layouts: 4.63 us -> none  [shards(): call(finish_kernel, [((count, width), BF16), ((count, width), BF16), ((wi...]
    transpose x0 -> x1, other arithmetic: none -> 3.8 us  [whole_layer(): jnp.transpose(sums[:3].astype(F32).reshape(3, width, size), (1, 0, 2))]
  transfers between devices with their start and end apart: 4 -> 0, of which waited for: 1 -> 0; matrix products, arithmetic and copies ran while one was open for 4% -> 0% of each run, Pallas kernels for 0% -> 0%
where the time goes in v2:
time: 152 us
  Pallas kernels  134 us (88%)
  local copies, waits for them, and re-layouts  10.6 us (7%)
  other arithmetic  6.64 us (4%)
    pallas_call x1, Pallas kernels, whole_layer(): pl.pallas_call(layer_kernel, out_shape=[jax.ShapeDtypeStruct((count, half...  134 us
    unnamed x7, local copies, waits for them, and re-layouts  4.29 us
    transpose x1, other arithmetic, whole_layer(): jnp.transpose(sums[:3].astype(F32).reshape(3, width, size), (1, 0, 2))  3.8 us

profile of v2, /device:TPU:0, one launch (start us, length us, event | category | flops | bytes accessed | tf_op | source)
XLA Modules:
  0.0 151.8 jit_solution(14278263122764383174)
XLA Ops:
  0.6 1.3 broadcast_in_dim_squeeze.3.lab_ref
  1.9 133.9 %shard_map.84 = (bf16[256,512]{1,0:T(8,128)(2,1)}, bf16[256,512]{1,0:T(8,128)(2,1)}, bf16[4,2,512,512]{3,2,1,0:T(8,128)(2,1)}) custom-call(bf16[256,512]{1,0:T(8,128)(2,1)} %bitcast.20, bf16[256,512]{1,0:T(8,128)(2,1)} %bitcast.21, bf16[3,1024,512]{2,1,0:T(8,128)(2,1)} %bitcast.17, bf16[512,1024]{1,0:T(8,128)(2,1)} %wo_ref.1, ...), custom_call_target="tpu_custom_call" | custom-call | tf_op jit(solution)/shard_map/pallas_call | solution.py:466
  135.8 2.8 %convert_bitcast_fusion.1 = f32[512,2,512]{2,0,1:T(8,128)} fusion(bf16[4,2,512,512]{3,2,1,0:T(8,128)(2,1)} %get-tuple-element.9), kind=kLoop, calls=%fused_computation.1 | loop fusion | flops 524288 | bytes 3145728 | tf_op jit(solution)/shard_map/reshape | solution.py:481
  138.7 2.1 %slice.6 = bf16[3,2,512,512]{3,2,1,0:T(8,128)(2,1)S(1)} slice(bf16[4,2,512,512]{3,2,1,0:T(8,128)(2,1)} %get-tuple-element.9), slice={[0:3], [0:2], [0:512], [0:512]} | slice | bytes 6291456 | tf_op jit(solution)/shard_map/slice | solution.py:480
  140.8 2.9 %copy.9 = f32[512,2,512]{0,2,1:T(8,128)} copy(f32[512,2,512]{2,0,1:T(8,128)} %convert_bitcast_fusion.1) | data formatting | bytes 4194304 | tf_op jit(solution)/shard_map/reshape | solution.py:481
  143.7 2.9 %copy.10 = f32[512,1024]{1,0:T(8,128)} copy(f32[512,1024]{0,1:T(8,128)} %bitcast.16) | data formatting | bytes 4194304
  146.5 0.0 copy-start.1
  146.5 0.0 copy-start
  146.5 3.8 %convert_bitcast_fusion = f32[1024,3,512]{2,0,1:T(8,128)} fusion(bf16[3,2,512,512]{3,2,1,0:T(8,128)(2,1)S(1)} %slice.6), kind=kLoop, calls=%fused_computation | loop fusion | flops 1572864 | bytes 9437184 | tf_op jit(solution)/shard_map/transpose | solution.py:480
  150.4 0.0 copy-done.1
  150.4 0.7 copy.13
  151.1 0.0 copy-done
  151.1 0.7 copy.14
Async XLA Ops:
  146.5 3.8 %copy-start.1 = (bf16[256,512]{1,0:T(8,128)(2,1)S(1)}, bf16[256,512]{1,0:T(8,128)(2,1)}, u32[]{:S(2)}) copy-start(bf16[256,512]{1,0:T(8,128)(2,1)} %get-tuple-element.7) | copy-start | bytes 786436
  146.5 4.5 %copy-start = (bf16[256,512]{1,0:T(8,128)(2,1)S(1)}, bf16[256,512]{1,0:T(8,128)(2,1)}, u32[]{:S(2)}) copy-start(bf16[256,512]{1,0:T(8,128)(2,1)} %get-tuple-element.8) | copy-start | bytes 786436

commit v3 on v2

--- a/solution.py
+++ b/solution.py
@@ -113,11 +113,11 @@
 
 
 def layer_kernel(
-    tok_ref, gro_ref, w3_ref, wo_ref, lab_ref,
-    att_out, tokgrad_out, res_out,
-    rows, grads, acc, packed, heads_in, marks, full, y, home,
+    tok_ref, gro_ref, w3_hbm, wo_hbm, lab_ref,
+    att_out, tokgrad_out, gwq_out, gwo_out,
+    w3_ref, wo_ref, rows, grads, acc, packed, heads_in, marks, full, y, home,
     part, from_core, chip_sum, from_outer, from_inner, res, x_send, x_recv, x_own, tok_out,
-    sx, rx, sl, rl, sa, ra, sb, rb, su, ru, so, ro, si, ri, sq, rq, sp, rp, sc, rc, st, rt, lsem,
+    sx, rx, sl, rl, sa, ra, sb, rb, su, ru, so, ro, si, ri, sq, rq, sp, rp, sc, rc, st, rt, lsem, wsem,
 ):
     z = lax.axis_index("ctx")
     x = lax.axis_index("tensor")
@@ -132,6 +132,12 @@
     peers = [lax.rem(z + d, 4) for d in range(1, 4)]
     sources = [lax.rem(z + 4 - d, 4) for d in range(1, 4)]
 
+    w_copies = [
+        pltpu.make_async_copy(w3_hbm, w3_ref, wsem.at[0]),
+        pltpu.make_async_copy(wo_hbm, wo_ref, wsem.at[1]),
+    ]
+    for copy in w_copies:
+        copy.start()
     barrier = pltpu.get_barrier_semaphore()
     for device in [{"ctx": p} for p in peers] + [x_dev, c_dev]:
         pl.semaphore_signal(barrier, inc=1, device_id=device, device_id_type=pl.DeviceIdType.MESH)
@@ -140,10 +146,13 @@
     def block(index, size):
         return pl.ds(pl.multiple_of(index * size, size), size)
 
-    x_copies = [
-        remote(tok_ref, rows.at[x], sx.at[0], rx.at[0], x_dev),
-        remote(gro_ref, grads.at[x], sx.at[1], rx.at[1], x_dev),
-    ]
+    pieces = 4
+    piece = count // pieces
+    x_copies = []
+    for r in range(pieces):
+        at = slice(r * piece, (r + 1) * piece)
+        x_copies.append(remote(tok_ref.at[at], rows.at[x, at], sx.at[r], rx.at[r], x_dev))
+    x_copies.append(remote(gro_ref, grads.at[x], sx.at[pieces], rx.at[pieces], x_dev))
     for copy in x_copies:
         copy.start()
     label_copies = []
@@ -155,38 +164,53 @@
     rows[x] = tok_ref[...]
     grads[x] = gro_ref[...]
     marks[z] = lab_ref[z]
+    for copy in w_copies:
+        copy.wait()
     for j in range(3):
         acc[j] = dot_general(tok_ref[...], w3_ref[j, block(x, half), :], 1, 0)
-    acc[3] = dot_general(gro_ref[...], wo_ref[:, block(x, half)], 1, 1)
 
     a_copies = []
-    for j in range(4):
-        if j == 0:
-            x_copies[0].wait_recv()
-        if j == 3:
-            x_copies[1].wait_recv()
-        if j < 3:
-            term = dot_general(rows[other_x], w3_ref[j, block(other_x, half), :], 1, 0)
-        else:
-            term = dot_general(grads[other_x], wo_ref[:, block(other_x, half)], 1, 1)
-        value = (acc[j] + term).astype(BF16)
-        for h in range(4):
-            packed[j, h] = value[:, h * HD : (h + 1) * HD]
+    for r in range(pieces):
+        at = slice(r * piece, (r + 1) * piece)
+        x_copies[r].wait_recv()
+        for j in range(3):
+            term = dot_general(rows[other_x, at, :], w3_ref[j, block(other_x, half), :], 1, 0)
+            value = (acc[j, at, :] + term).astype(BF16)
+            for h in range(4):
+                packed[h, j, at, :] = value[:, h * HD : (h + 1) * HD]
+        spot = pl.ds(pl.multiple_of(z * count + r * piece, piece), piece)
         for d in range(3):
             copy = remote(
-                packed.at[j, peers[d]],
-                heads_in.at[j, block(z, count), :],
-                sa.at[j, d],
-                ra.at[j, d],
+                packed.at[peers[d], 0:3, at, :],
+                heads_in.at[0:3, spot, :],
+                sa.at[r, d],
+                ra.at[r, d],
                 {"ctx": peers[d]},
             )
             copy.start()
             a_copies.append(copy)
-        heads_in[j, block(z, count), :] = packed[j, z]
+    acc[3] = dot_general(gro_ref[...], wo_ref[:, block(x, half)], 1, 1)
+    x_copies[pieces].wait_recv()
+    term = dot_general(grads[other_x], wo_ref[:, block(other_x, half)], 1, 1)
+    value = (acc[3] + term).astype(BF16)
+    for h in range(4):
+        packed[h, 3] = value[:, h * HD : (h + 1) * HD]
+    for d in range(3):
+        copy = remote(
+            packed.at[peers[d], 3],
+            heads_in.at[3, block(z, count), :],
+            sa.at[pieces, d],
+            ra.at[pieces, d],
+            {"ctx": peers[d]},
+        )
+        copy.start()
+        a_copies.append(copy)
+    for j in range(4):
+        heads_in[j, block(z, count), :] = packed[z, j]
 
     for copy in label_copies:
         copy.wait_recv()
-    for copy in a_copies[:9]:
+    for copy in a_copies[: 3 * pieces]:
         copy.wait_recv()
     keys = heads_in[1]
     values = heads_in[2]
@@ -217,7 +241,7 @@
         if d < 3:
             send_back(3, d)
     home[3, z] = y[3, block(z, count), :]
-    for copy in a_copies[9:]:
+    for copy in a_copies[3 * pieces :]:
         copy.wait_recv()
     grad_keys = grad_values = None
     for d in range(4):
@@ -254,7 +278,62 @@
             return dot_general(grad, grads[f], 0, 0)
         return dot_general(rows[f], grad, 0, 0)
 
-    for u in units:
+    inner = jnp.logical_or(z == 1, z == 2)
+    side = z // 2
+    inner_of_outer = jnp.where(z == 0, 1, 2)
+    outer_dev = {"ctx": jnp.where(z == 1, 0, 3)}
+    inner_dev = {"ctx": jnp.where(z == 1, 2, 1)}
+    chunks = 4
+    rows_at = half // 2 // chunks
+    steps = [(u, k) for u in units for k in range(chunks)]
+
+    def chunk(which, k):
+        return pl.ds(pl.multiple_of(which * (half // 2) + k * rows_at, rows_at), rows_at)
+
+    def outer_send(n, which):
+        u, k = steps[n]
+        at = chunk(which, k)
+        q = n * 2 + which
+        return remote(
+            chip_sum.at[u, at, :], from_outer.at[u, at, :], so.at[q], ro.at[q], {"ctx": inner_of_outer}
+        )
+
+    def from_outer_copy(n, which):
+        u, k = steps[n]
+        at = chunk(which, k)
+        q = n * 2 + which
+        return remote(chip_sum.at[u, at, :], from_outer.at[u, at, :], so.at[q], ro.at[q], outer_dev)
+
+    def inner_partial(n, which):
+        u, k = steps[n]
+        at = chunk(which, k)
+        return remote(chip_sum.at[u, at, :], from_inner.at[u, at, :], si.at[n], ri.at[n], inner_dev)
+
+    def inner_result(n, which):
+        u, k = steps[n]
+        at = chunk(which, k)
+        return remote(res.at[u, c, at, :], res.at[u, c, at, :], sq.at[n], rq.at[n], inner_dev)
+
+    def outer_result(n, which, device):
+        u, k = steps[n]
+        at = chunk(which, k)
+        q = n * 2 + which
+        return remote(res.at[u, c, at, :], res.at[u, c, at, :], sp.at[q], rp.at[q], device)
+
+    def core_result(n, which):
+        u, k = steps[n]
+        at = chunk(which, k)
+        q = n * 2 + which
+        return remote(res.at[u, c, at, :], res.at[u, c, at, :], sc.at[q], rc.at[q], c_dev)
+
+    def core_result_in(n, which):
+        u, k = steps[n]
+        at = chunk(which, k)
+        q = n * 2 + which
+        return remote(res.at[u, other_c, at, :], res.at[u, other_c, at, :], sc.at[q], rc.at[q], c_dev)
+
+    near, far = side, 1 - side
+    def start_unit(u):
         for copy in b_at[u]:
             copy.wait_recv()
         grad = jnp.concatenate([home[u, h] for h in range(4)], axis=1)
@@ -263,69 +342,22 @@
         u_copies[u].start()
         chip_sum[u] = unit_term(u, grad, c).astype(BF16)
 
-    inner = jnp.logical_or(z == 1, z == 2)
-    side = z // 2
-    inner_of_outer = jnp.where(z == 0, 1, 2)
-    outer_dev = {"ctx": jnp.where(z == 1, 0, 3)}
-    inner_dev = {"ctx": jnp.where(z == 1, 2, 1)}
-    steps = [(u, k) for u in units for k in range(2)]
-
-    def chunk(which, k):
-        return pl.ds(pl.multiple_of(which * 256 + k * 128, 128), 128)
-
-    def outer_send(n, which):
-        u, k = steps[n]
-        at = chunk(which, k)
-        q = n * 2 + which
-        return remote(
-            chip_sum.at[u, at, :], from_outer.at[u, at, :], so.at[q], ro.at[q], {"ctx": inner_of_outer}
-        )
-
-    def from_outer_copy(n, which):
-        u, k = steps[n]
-        at = chunk(which, k)
-        q = n * 2 + which
-        return remote(chip_sum.at[u, at, :], from_outer.at[u, at, :], so.at[q], ro.at[q], outer_dev)
-
-    def inner_partial(n, which):
-        u, k = steps[n]
-        at = chunk(which, k)
-        return remote(chip_sum.at[u, at, :], from_inner.at[u, at, :], si.at[n], ri.at[n], inner_dev)
-
-    def inner_result(n, which):
-        u, k = steps[n]
-        at = chunk(which, k)
-        return remote(res.at[u, c, at, :], res.at[u, c, at, :], sq.at[n], rq.at[n], inner_dev)
-
-    def outer_result(n, which, device):
-        u, k = steps[n]
-        at = chunk(which, k)
-        q = n * 2 + which
-        return remote(res.at[u, c, at, :], res.at[u, c, at, :], sp.at[q], rp.at[q], device)
-
-    def core_result(n, which):
-        u, k = steps[n]
-        at = chunk(which, k)
-        q = n * 2 + which
-        return remote(res.at[u, c, at, :], res.at[u, c, at, :], sc.at[q], rc.at[q], c_dev)
-
-    def core_result_in(n, which):
-        u, k = steps[n]
-        at = chunk(which, k)
-        q = n * 2 + which
-        return remote(res.at[u, other_c, at, :], res.at[u, other_c, at, :], sc.at[q], rc.at[q], c_dev)
-
-    near, far = side, 1 - side
-    for u in units:
+    def send_unit(u):
         u_copies[u].wait_recv()
         chip_sum[u] = (chip_sum[u].astype(F32) + from_core[u].astype(F32)).astype(BF16)
 
         @pl.when(jnp.logical_not(inner))
-        def _(u=u):
-            for k in range(2):
+        def _():
+            for k in range(chunks):
                 n = steps.index((u, k))
                 outer_send(n, far).start()
                 outer_send(n, near).start()
+
+    start_unit(units[0])
+    for before, u in zip(units, units[1:]):
+        start_unit(u)
+        send_unit(before)
+    send_unit(units[-1])
 
     t_copies = []
 
@@ -340,69 +372,91 @@
             total = term if total is None else total + term
         return total
 
-    for t in range(2):
-        x_send[t] = token_term(t, other_x).astype(BF16)
-        t_copies.append(remote(x_send.at[t], x_recv.at[t], st.at[t], rt.at[t], x_dev))
-        t_copies[t].start()
-    for t in range(2):
-        x_own[t] = token_term(t, x)
+    def token_piece(i):
+        t = i % 2
+        if i < 2:
+            x_send[t] = token_term(t, other_x).astype(BF16)
+            t_copies.append(remote(x_send.at[t], x_recv.at[t], st.at[t], rt.at[t], x_dev))
+            t_copies[t].start()
+        else:
+            x_own[t] = token_term(t, x)
 
     count_steps = len(steps)
     lag = 2
-
-    @pl.when(inner)
-    def _():
-        def relay(n):
-            inner_result(n, far).wait_recv()
-            outer_result(n, far, outer_dev).start()
-            core_result(n, far).start()
-
-        for n in range(count_steps):
-            u, k = steps[n]
-            far_at, near_at = chunk(far, k), chunk(near, k)
-            from_outer_copy(n, far).wait_recv()
-            chip_sum[u, far_at, :] = (
-                chip_sum[u, far_at, :].astype(F32) + from_outer[u, far_at, :].astype(F32)
-            ).astype(BF16)
-            inner_partial(n, far).start()
-            from_outer_copy(n, near).wait_recv()
-            inner_partial(n, near).wait_recv()
-            res[u, c, near_at, :] = (
-                chip_sum[u, near_at, :].astype(F32)
-                + from_outer[u, near_at, :].astype(F32)
-                + from_inner[u, near_at, :].astype(F32)
-            ).astype(BF16)
-            inner_result(n, near).start()
-            outer_result(n, near, outer_dev).start()
-            core_result(n, near).start()
-            if n >= lag:
-                relay(n - lag)
-        for n in range(count_steps - lag, count_steps):
-            relay(n)
-        for n in range(count_steps):
-            inner_partial(n, far).wait_send()
-            inner_result(n, near).wait_send()
-            for which in (near, far):
-                outer_result(n, which, outer_dev).wait_send()
-
-    @pl.when(jnp.logical_not(inner))
-    def _():
-        back = {"ctx": inner_of_outer}
-        for n in range(count_steps):
-            outer_result(n, near, back).wait_recv()
-            core_result(n, near).start()
-            if n >= lag:
-                outer_result(n - lag, far, back).wait_recv()
-                core_result(n - lag, far).start()
-        for n in range(count_steps - lag, count_steps):
-            outer_result(n, far, back).wait_recv()
-            core_result(n, far).start()
-        for n in range(count_steps):
-            for which in (near, far):
-                outer_send(n, which).wait_send()
+    back = {"ctx": inner_of_outer}
+
+    def relay(n):
+        inner_result(n, far).wait_recv()
+        outer_result(n, far, outer_dev).start()
+        core_result(n, far).start()
+
+    def inner_step(n):
+        u, k = steps[n]
+        far_at, near_at = chunk(far, k), chunk(near, k)
+        from_outer_copy(n, far).wait_recv()
+        chip_sum[u, far_at, :] = (
+            chip_sum[u, far_at, :].astype(F32) + from_outer[u, far_at, :].astype(F32)
+        ).astype(BF16)
+        inner_partial(n, far).start()
+        from_outer_copy(n, near).wait_recv()
+        inner_partial(n, near).wait_recv()
+        res[u, c, near_at, :] = (
+            chip_sum[u, near_at, :].astype(F32)
+            + from_outer[u, near_at, :].astype(F32)
+            + from_inner[u, near_at, :].astype(F32)
+        ).astype(BF16)
+        inner_result(n, near).start()
+        outer_result(n, near, outer_dev).start()
+        core_result(n, near).start()
+        if n >= lag:
+            relay(n - lag)
+
+    def outer_take(n, which):
+        outer_result(n, which, back).wait_recv()
+        core_result(n, which).start()
+
+    def outer_step(n):
+        outer_take(n, near)
+        if n >= lag:
+            outer_take(n - lag, far)
+
+    edges = [0, 2, 4, 6, 8, count_steps]
+    for i, (first, last) in enumerate(zip(edges, edges[1:])):
+        final = last == count_steps
+
+        @pl.when(inner)
+        def _():
+            for n in range(first, last):
+                inner_step(n)
+            if final:
+                for n in range(count_steps - lag, count_steps):
+                    relay(n)
+                for n in range(count_steps):
+                    inner_partial(n, far).wait_send()
+                    inner_result(n, near).wait_send()
+                    for which in (near, far):
+                        outer_result(n, which, outer_dev).wait_send()
+
+        @pl.when(jnp.logical_not(inner))
+        def _():
+            for n in range(first, last):
+                outer_step(n)
+            if final:
+                for n in range(count_steps - lag, count_steps):
+                    outer_take(n, far)
+                for n in range(count_steps):
+                    for which in (near, far):
+                        outer_send(n, which).wait_send()
+
+        if not final:
+            token_piece(i)
+
+    def result_out(u, f, sem):
+        target = gwo_out.at[:, block(f, half)] if u == 3 else gwq_out.at[u, f]
+        return pltpu.make_async_copy(res.at[u, f], target, sem)
 
     own_out = [
-        pltpu.make_async_copy(res.at[u, c], res_out.at[u, c], lsem.at[u]) for u in units
+        result_out(u, c, lsem.at[u]) for u in units
     ]
     for copy in own_out:
         copy.start()
@@ -417,10 +471,10 @@
         copy.start()
     other_out = []
     for i, u in enumerate(units):
-        for n in (2 * i, 2 * i + 1):
+        for n in range(chunks * i, chunks * (i + 1)):
             for which in (near, far):
                 core_result_in(n, which).wait_recv()
-        copy = pltpu.make_async_copy(res.at[u, other_c], res_out.at[u, other_c], lsem.at[4 + u])
+        copy = result_out(u, other_c, lsem.at[4 + u])
         copy.start()
         other_out.append(copy)
     for copy in own_out + token_out + other_out:
@@ -440,6 +494,8 @@
     dma = pltpu.SemaphoreType.DMA
     square = (4, half, size)
     scratch = [
+        pltpu.VMEM((3, width, size), BF16),
+        pltpu.VMEM((size, width), BF16),
         pltpu.VMEM((2, count, half), BF16),
         pltpu.VMEM((2, count, half), BF16),
         pltpu.VMEM((4, count, size), F32),
@@ -460,25 +516,26 @@
         pltpu.VMEM((2, count, half), F32),
         pltpu.VMEM((2, count, half), BF16),
     ]
-    for shape in ((2,), (3,), (4, 3), (4, 3), (4,), (16,), (8,), (8,), (16,), (16,), (2,)):
+    for shape in ((5,), (3,), (5, 3), (4, 3), (4,), (32,), (16,), (16,), (32,), (32,), (2,)):
         scratch += [dma(shape), dma(shape)]
-    scratch.append(dma((10,)))
-    attended, grad_tokens, sums = pl.pallas_call(
+    scratch += [dma((10,)), dma((2,))]
+    attended, grad_tokens, sum_qkv, sum_out = pl.pallas_call(
         layer_kernel,
         out_shape=[
             jax.ShapeDtypeStruct((count, half), BF16),
             jax.ShapeDtypeStruct((count, half), BF16),
-            jax.ShapeDtypeStruct((4, 2, half, size), BF16),
+            jax.ShapeDtypeStruct((3, 2, half, size), BF16),
+            jax.ShapeDtypeStruct((size, width), BF16),
         ],
-        in_specs=[VMEM_SPEC] * 5,
-        out_specs=[any_spec] * 3,
+        in_specs=[VMEM_SPEC] * 2 + [any_spec] * 2 + [VMEM_SPEC],
+        out_specs=[any_spec] * 4,
         scratch_shapes=scratch,
         compiler_params=pltpu.CompilerParams(
             collective_id=0, has_side_effects=True, vmem_limit_bytes=56 * 2**20
         ),
     )(tokens[0], grad_out[0], jnp.transpose(w_qkv, (1, 0, 2)), w_out, labels[0][:, None, :])
-    grad_w_qkv = jnp.transpose(sums[:3].astype(F32).reshape(3, width, size), (1, 0, 2))
-    grad_w_out = jnp.transpose(sums[3].astype(F32), (1, 0, 2)).reshape(size, width)
+    grad_w_qkv = jnp.transpose(sum_qkv.astype(F32).reshape(3, width, size), (1, 0, 2))
+    grad_w_out = sum_out.astype(F32)
     return attended[None], grad_tokens[None], grad_w_qkv, grad_w_out
 
 

time: 152 us -> 150 us (0.987)
  local copies, waits for them, and re-layouts: 10.6 us -> 2.7 us
  Pallas kernels: 134 us -> 139 us
    pallas_call x1, Pallas kernels: 134 us -> 139 us  [whole_layer(): pl.pallas_call(layer_kernel, out_shape=[jax.ShapeDtypeStruct((count, half...]
    reshape x1 -> x0, local copies, waits for them, and re-layouts: 2.88 us -> none  [whole_layer(): jnp.transpose(sums[3].astype(F32), (1, 0, 2)).reshape(size, width)]
    unnamed x7 -> x8, local copies, waits for them, and re-layouts: 4.29 us -> 1.42 us
    reshape x1 -> x0, other arithmetic: 2.84 us -> none  [whole_layer(): jnp.transpose(sums[3].astype(F32), (1, 0, 2)).reshape(size, width)]
    slice x1 -> x0, local copies, waits for them, and re-layouts: 2.09 us -> none  [whole_layer(): sums[:3].astype(F32).reshape(3, width, size)]
    transpose x1, other arithmetic: 3.8 us -> 5.58 us  [whole_layer(): jnp.transpose(sum_qkv.astype(F32).reshape(3, width, size), (1, 0, 2))]
    convert_element_type x0 -> x1, other arithmetic: none -> 1.57 us  [whole_layer(): grad_w_out = sum_out.astype(F32)]
where the time goes in v3:
time: 150 us
  Pallas kernels  139 us (93%)
  other arithmetic  7.14 us (5%)
  local copies, waits for them, and re-layouts  2.7 us (2%)
    pallas_call x1, Pallas kernels, whole_layer(): pl.pallas_call(layer_kernel, out_shape=[jax.ShapeDtypeStruct((count, half...  139 us
    transpose x1, other arithmetic, whole_layer(): jnp.transpose(sum_qkv.astype(F32).reshape(3, width, size), (1, 0, 2))  5.58 us

profile of v3, /device:TPU:0, one launch (start us, length us, event | category | flops | bytes accessed | tf_op | source)
XLA Modules:
  0.0 149.8 jit_solution(13177453018553694316)
XLA Ops:
  0.6 1.3 broadcast_in_dim_squeeze.3.lab_ref
  1.9 139.3 %shard_map.84 = (bf16[256,512]{1,0:T(8,128)(2,1)}, bf16[256,512]{1,0:T(8,128)(2,1)}, bf16[3,2,512,512]{3,2,1,0:T(8,128)(2,1)}, bf16[512,1024]{1,0:T(8,128)(2,1)}) custom-call(bf16[256,512]{1,0:T(8,128)(2,1)} %bitcast.13, bf16[256,512]{1,0:T(8,128)(2,1)} %bitcast.14, bf16[3,1024,512]{2,1,0:T(8,128)(2,1)} %bitcast.10, bf16[512,1024]{1,0:T(8,128)(2,1)} %wo_hbm.1, ...), custom_call_target="tpu_custom_call" | custom-call | tf_op jit(solution)/shard_map/pallas_call | solution.py:522
  141.2 0.0 copy-start
  141.2 5.6 %convert_bitcast_fusion = f32[1024,3,512]{2,0,1:T(8,128)} fusion(bf16[3,2,512,512]{3,2,1,0:T(8,128)(2,1)} %get-tuple-element.10), kind=kLoop, calls=%fused_computation | loop fusion | flops 1572864 | bytes 9437184 | tf_op jit(solution)/shard_map/transpose | solution.py:537
  146.8 0.0 copy-start.2
  146.8 0.0 copy-start.1
  146.8 0.0 copy-done
  146.8 1.6 %convert_element_type.4 = f32[512,1024]{1,0:T(8,128)} convert(bf16[512,1024]{1,0:T(8,128)(2,1)S(1)} %copy-done) | non-fusion elementwise | flops 524288 | bytes 3145728 | tf_op jit(solution)/shard_map/convert_element_type | solution.py:538
  148.4 0.0 copy-done.2
  148.4 0.7 copy.11
  149.1 0.0 copy-done.1
  149.1 0.7 copy.12
Async XLA Ops:
  141.2 5.6 %copy-start = (bf16[512,1024]{1,0:T(8,128)(2,1)S(1)}, bf16[512,1024]{1,0:T(8,128)(2,1)}, u32[]{:S(2)}) copy-start(bf16[512,1024]{1,0:T(8,128)(2,1)} %get-tuple-element.11) | copy-start | bytes 3145732
  146.8 1.6 %copy-start.2 = (bf16[256,512]{1,0:T(8,128)(2,1)S(1)}, bf16[256,512]{1,0:T(8,128)(2,1)}, u32[]{:S(2)}) copy-start(bf16[256,512]{1,0:T(8,128)(2,1)} %get-tuple-element.8) | copy-start | bytes 786436
  146.8 2.3 %copy-start.1 = (bf16[256,512]{1,0:T(8,128)(2,1)S(1)}, bf16[256,512]{1,0:T(8,128)(2,1)}, u32[]{:S(2)}) copy-start(bf16[256,512]{1,0:T(8,128)(2,1)} %get-tuple-element.9) | copy-start | bytes 786436

commit v4 on v3

--- a/solution.py
+++ b/solution.py
@@ -283,7 +283,7 @@
     inner_of_outer = jnp.where(z == 0, 1, 2)
     outer_dev = {"ctx": jnp.where(z == 1, 0, 3)}
     inner_dev = {"ctx": jnp.where(z == 1, 2, 1)}
-    chunks = 4
+    chunks = 1
     rows_at = half // 2 // chunks
     steps = [(u, k) for u in units for k in range(chunks)]
 
@@ -382,7 +382,7 @@
             x_own[t] = token_term(t, x)
 
     count_steps = len(steps)
-    lag = 2
+    lag = 1
     back = {"ctx": inner_of_outer}
 
     def relay(n):
@@ -420,7 +420,7 @@
         if n >= lag:
             outer_take(n - lag, far)
 
-    edges = [0, 2, 4, 6, 8, count_steps]
+    edges = [0, 0, 1, 2, 3, count_steps]
     for i, (first, last) in enumerate(zip(edges, edges[1:])):
         final = last == count_steps
 

time: 150 us -> 133 us (0.89)
  Pallas kernels: 139 us -> 122 us
    pallas_call x1, Pallas kernels: 139 us -> 122 us  [whole_layer(): pl.pallas_call(layer_kernel, out_shape=[jax.ShapeDtypeStruct((count, half...]
where the time goes in v4:
time: 133 us
  Pallas kernels  122 us (92%)
  other arithmetic  7.14 us (5%)
  local copies, waits for them, and re-layouts  2.7 us (2%)
    pallas_call x1, Pallas kernels, whole_layer(): pl.pallas_call(layer_kernel, out_shape=[jax.ShapeDtypeStruct((count, half...  122 us
    transpose x1, other arithmetic, whole_layer(): jnp.transpose(sum_qkv.astype(F32).reshape(3, width, size), (1, 0, 2))  5.58 us

profile of v4, /device:TPU:0, one launch (start us, length us, event | category | flops | bytes accessed | tf_op | source)
XLA Modules:
  0.0 132.7 jit_solution(6985283949453979097)
XLA Ops:
  0.6 1.3 broadcast_in_dim_squeeze.3.lab_ref
  1.9 122.2 %shard_map.84 = (bf16[256,512]{1,0:T(8,128)(2,1)}, bf16[256,512]{1,0:T(8,128)(2,1)}, bf16[3,2,512,512]{3,2,1,0:T(8,128)(2,1)}, bf16[512,1024]{1,0:T(8,128)(2,1)}) custom-call(bf16[256,512]{1,0:T(8,128)(2,1)} %bitcast.13, bf16[256,512]{1,0:T(8,128)(2,1)} %bitcast.14, bf16[3,1024,512]{2,1,0:T(8,128)(2,1)} %bitcast.10, bf16[512,1024]{1,0:T(8,128)(2,1)} %wo_hbm.1, ...), custom_call_target="tpu_custom_call" | custom-call | tf_op jit(solution)/shard_map/pallas_call | solution.py:522
  124.1 0.0 copy-start
  124.1 5.6 %convert_bitcast_fusion = f32[1024,3,512]{2,0,1:T(8,128)} fusion(bf16[3,2,512,512]{3,2,1,0:T(8,128)(2,1)} %get-tuple-element.10), kind=kLoop, calls=%fused_computation | loop fusion | flops 1572864 | bytes 9437184 | tf_op jit(solution)/shard_map/transpose | solution.py:537
  129.7 0.0 copy-start.2
  129.7 0.0 copy-start.1
  129.7 0.0 copy-done
  129.7 1.6 %convert_element_type.4 = f32[512,1024]{1,0:T(8,128)} convert(bf16[512,1024]{1,0:T(8,128)(2,1)S(1)} %copy-done) | non-fusion elementwise | flops 524288 | bytes 3145728 | tf_op jit(solution)/shard_map/convert_element_type | solution.py:538
  131.3 0.0 copy-done.2
  131.3 0.7 copy.11
  132.0 0.0 copy-done.1
  132.0 0.7 copy.12
Async XLA Ops:
  124.1 5.6 %copy-start = (bf16[512,1024]{1,0:T(8,128)(2,1)S(1)}, bf16[512,1024]{1,0:T(8,128)(2,1)}, u32[]{:S(2)}) copy-start(bf16[512,1024]{1,0:T(8,128)(2,1)} %get-tuple-element.11) | copy-start | bytes 3145732
  129.7 1.6 %copy-start.2 = (bf16[256,512]{1,0:T(8,128)(2,1)S(1)}, bf16[256,512]{1,0:T(8,128)(2,1)}, u32[]{:S(2)}) copy-start(bf16[256,512]{1,0:T(8,128)(2,1)} %get-tuple-element.8) | copy-start | bytes 786436
  129.7 2.3 %copy-start.1 = (bf16[256,512]{1,0:T(8,128)(2,1)S(1)}, bf16[256,512]{1,0:T(8,128)(2,1)}, u32[]{:S(2)}) copy-start(bf16[256,512]{1,0:T(8,128)(2,1)} %get-tuple-element.9) | copy-start | bytes 786436
